TPU v7x, 32 devices: a whole 2x2x4 slice. The times are simulated.
32 devices in a mesh: groups: 2 (over x), frame: 16 (over z, y, core).
Axes of the slice: x: 2, y: 2, z: 4, core: 2. Of those that a mesh axis runs over, the one named last changes fastest.
Arguments:
- lowres: bfloat16 [32, 64, 128], P(('groups', 'frame')), parts along dimension 0, may hold values from -6 to 6
- noisy: bfloat16 [32, 8, 64, 128], P(('groups', 'frame')), parts along dimension 0, may hold values from -6 to 6
- starts: int32 [8], P('groups'), parts along dimension 0, may hold values from 0 to 8, as said below
- blend: int32 [8, 8], P('groups'), parts along dimension 0, may hold values from 1 to 4
- assign: int32 [32], P('groups'), parts along dimension 0, may hold values from 0 to 15, each once
- base_w: bfloat16 [3, 128, 128], replicated, may hold values from -0.3125 to 0.3125
- cond_w: bfloat16 [128, 128], replicated, may hold values from -0.5 to 0.5
- noise_w: bfloat16 [128, 128], replicated, may hold values from -0.5 to 0.5
- gains: float32 [3, 128], replicated, may hold values from 0.25 to 1.75
- tconv: float32 [3, 3, 128], replicated, may hold values from -3 to 3
- mlp_in: bfloat16 [3, 128, 512], replicated, may hold values from -0.5 to 0.5
- mlp_out: bfloat16 [3, 512, 128], replicated, may hold values from -0.25 to 0.25
Outputs:
- video: bfloat16 [32, 256, 128], P(('groups', 'frame')), parts along dimension 0
There are 2 independent parts, one for each index of `groups`. A program takes and returns all parts, laid end to end along the dimension named above; an argument that names none is the same for every part. Nothing has to cross between parts.
Inputs may be any that keep to these rules, and one draw needn't show every extreme that they name: Window k covers frames starts[k] to starts[k] + 7; every frame lies in some window; the first window starts at 0 and the last at 8.
All inputs are finite; a program needn't handle non-finite values.
Results may differ from a plain program's by a relative error of at most 0.0059.
Values may be sent and summed in bfloat16 or wider, within the bound.
No kernel may reach another device: no remote copies, remote signals or barrier semaphores. Data moves between devices by JAX's collectives and lax.ppermute only.
A program may use at most 64 MiB of HBM per device.

v0:
```python
import jax
import jax.numpy as jnp
from jax import lax
from jax.sharding import PartitionSpec as P

TILES = 4


def padded_2(cells, sides, width):
    for axis, dim in sides:
        count = lax.axis_size(axis)
        ends = count - 1
        head = lax.slice_in_dim(cells, 0, width, axis=dim)
        tail = lax.slice_in_dim(cells, cells.shape[dim] - width, cells.shape[dim], axis=dim)
        cells = jnp.concatenate(
            [
                lax.ppermute(tail, axis, [(i, (i + 1) % count) for i in range(ends)]),
                cells,
                lax.ppermute(head, axis, [((i + 1) % count, i) for i in range(ends)]),
            ],
            axis=dim,
        )
    return cells


def refine_block(cond, noisy_item, cond_w, noise_w, gains, tconv, mlp_in, mlp_out):
    frame_count, positions, channels = cond.shape
    row_count = frame_count * positions
    state = jnp.dot(cond.reshape(row_count, channels), cond_w, preferred_element_type=jnp.float32)
    state = state + jnp.dot(
        noisy_item.reshape(row_count, channels), noise_w, preferred_element_type=jnp.float32
    )
    for layer_id in range(gains.shape[0]):
        inverse = lax.rsqrt(jnp.mean(state * state, axis=-1, keepdims=True) + 1e-06)
        normed = (state * inverse * gains[layer_id]).reshape(frame_count, positions, channels)
        zeros_frame = jnp.zeros_like(normed[:1])
        before = jnp.concatenate([zeros_frame, normed[:-1]], 0)
        behind = jnp.concatenate([normed[1:], zeros_frame], 0)
        mixed_rows = (
            normed
            + tconv[layer_id, 0] * before
            + tconv[layer_id, 1] * normed
            + tconv[layer_id, 2] * behind
        )
        mixed_rows = mixed_rows.reshape(row_count, channels).astype(jnp.bfloat16)
        hidden = jax.nn.silu(
            jnp.dot(mixed_rows, mlp_in[layer_id], preferred_element_type=jnp.float32)
        ).astype(jnp.bfloat16)
        state = state + jnp.dot(hidden, mlp_out[layer_id], preferred_element_type=jnp.float32)
    return state.astype(jnp.bfloat16).reshape(frame_count, positions, channels)


def refine(cond, noisy_item, cond_w, noise_w, gains, tconv, mlp_in, mlp_out):
    frame_count, positions, channels = cond.shape
    block_count = positions // positions
    cond_blocks = jnp.transpose(
        cond.reshape(frame_count, block_count, positions, channels), (1, 0, 2, 3)
    )
    noisy_blocks = jnp.transpose(
        noisy_item.reshape(frame_count, block_count, positions, channels), (1, 0, 2, 3)
    )

    def one_block(pair):
        return refine_block(pair[0], pair[1], cond_w, noise_w, gains, tconv, mlp_in, mlp_out)

    outputs = lax.map(one_block, (cond_blocks, noisy_blocks))
    return jnp.transpose(outputs, (1, 0, 2, 3)).reshape(frame_count, positions, channels)


def on_device(
    lowres, noisy, starts, blend, assign, base_w, cond_w, noise_w, gains, tconv, mlp_in, mlp_out
):
    frame_total = assign.shape[0]
    window_len = noisy.shape[1]
    tile_pos = noisy.shape[2]
    channels = noisy.shape[3]
    low_pos = lowres.shape[1] // TILES
    padded = padded_2(lowres, (("frame", 0),), 1)
    total = jnp.dot(padded[0], base_w[0], preferred_element_type=jnp.float32)
    total = total + jnp.dot(padded[1], base_w[1], preferred_element_type=jnp.float32)
    total = total + jnp.dot(padded[2], base_w[2], preferred_element_type=jnp.float32)
    base_frame = (lowres[0].astype(jnp.float32) + jax.nn.silu(total)).astype(jnp.bfloat16)
    own_index = lax.axis_index("frame")
    item_id = assign[own_index]
    own_start = starts[item_id // TILES]
    tile_rows = base_frame.reshape(TILES, low_pos * channels)
    picker = (assign[:, None] % TILES == jnp.arange(TILES, dtype=jnp.int32)[None, :]).astype(
        jnp.bfloat16
    )
    outgoing = jnp.dot(picker, tile_rows, preferred_element_type=jnp.float32).astype(jnp.bfloat16)
    outgoing = outgoing.reshape(frame_total, low_pos, channels)
    gathered = lax.all_to_all(outgoing, "frame", split_axis=0, concat_axis=0, tiled=True)
    window_tiles = lax.dynamic_slice_in_dim(gathered, own_start, window_len, 0)
    cond = jnp.repeat(window_tiles, 4, axis=1)
    refined = refine(cond, noisy[0], cond_w, noise_w, gains, tconv, mlp_in, mlp_out)
    source_window = assign // TILES
    source_tile = assign % TILES
    placed = jnp.zeros((frame_total, tile_pos, channels), jnp.bfloat16)
    placed = lax.dynamic_update_slice_in_dim(placed, refined, own_start, 0)
    received = lax.all_to_all(placed, "frame", split_axis=0, concat_axis=0, tiled=True)
    offset = own_index - starts[source_window]
    inside = (offset >= 0) & (offset < window_len)
    clipped = jnp.clip(offset, 0, window_len - 1)
    factor = jnp.where(inside, blend[source_window, clipped], 0).astype(jnp.float32)
    tile_match = (source_tile[None, :] == jnp.arange(TILES, dtype=jnp.int32)[:, None]).astype(
        jnp.float32
    )
    blend_matrix = tile_match * factor[None, :]
    weighted = jnp.dot(
        blend_matrix.astype(jnp.bfloat16),
        received.reshape(frame_total, tile_pos * channels),
        preferred_element_type=jnp.float32,
    )
    denom = jnp.sum(blend_matrix, axis=1)
    video = weighted / denom[:, None]
    return video.reshape(1, TILES * tile_pos, channels).astype(jnp.bfloat16)


def solution(mesh):
    in_specs = (
        P(("groups", "frame"), None, None),
        P(("groups", "frame"), None, None, None),
        P("groups"),
        P("groups", None),
        P("groups"),
        P(),
        P(),
        P(),
        P(),
        P(),
        P(),
        P(),
    )
    out_specs = P(("groups", "frame"), None, None)
    return jax.shard_map(
        on_device, mesh=mesh, in_specs=in_specs, out_specs=out_specs, check_vma=False
    )
```

profile of v0, /device:TPU:0, one launch (start us, length us, event | category | flops | bytes accessed | tf_op | source)
XLA Modules:
  0.0 52.0 jit_solution(3728004417824354756)
XLA Ops:
  0.0 1.4 %collective-permute-start.1 = (bf16[1,64,128]{2,1,0:T(8,128)(2,1)}, bf16[1,64,128]{2,1,0:T(8,128)(2,1)S(1)}, u32[]{:S(2)}, u32[]{:S(2)}) collective-permute-start(bf16[1,64,128]{2,1,0:T(8,128)(2,1)} %param.12), channel_id=1, source_target_pairs={{1,0},{2,1},{3,2},{4,3},{5,4},{6,5},{7,6},{8,7},{9,8},{10,9},{11,1... | collective-permute-start | bytes 49160 | tf_op jit(solution)/shard_map/ppermute | solution.py:19
  1.4 3.0 %collective-permute-start = (bf16[1,64,128]{2,1,0:T(8,128)(2,1)}, bf16[1,64,128]{2,1,0:T(8,128)(2,1)S(1)}, u32[]{:S(2)}, u32[]{:S(2)}) collective-permute-start(bf16[1,64,128]{2,1,0:T(8,128)(2,1)} %param.12), channel_id=1, source_target_pairs={{0,1},{1,2},{2,3},{3,4},{4,5},{5,6},{6,7},{7,8},{8,9},{9,10},{10,1... | collective-permute-start | bytes 49160 | tf_op jit(solution)/shard_map/ppermute | solution.py:17
  4.5 0.7 %compare_select_fusion.1 = (s32[16]{0:T(128)S(1)}, s32[16]{0:T(128)S(1)}) fusion(s32[16]{0:T(128)} %param.16), kind=kLoop, calls=%fused_computation.58 | loop fusion | flops 352 | bytes 192 | tf_op jit(solution)/shard_map/select_n | solution.py:101
  5.1 0.9 %fusion.29 = f32[64,128]{1,0:T(8,128)S(1)} fusion(bf16[3,128,128]{2,1,0:T(8,128)(2,1)} %param.17, bf16[1,64,128]{2,1,0:T(8,128)(2,1)} %param.12), kind=kOutput, calls=%fused_computation.44 | convolution fusion | flops 2097152 | bytes 81920 | tf_op jit(solution)/shard_map/dot_general | solution.py:80
  6.1 0.6 %copy-done.11 = s32[16]{0:T(128)S(1)} copy-done((s32[16]{0:T(128)S(1)}, s32[16]{0:T(128)}, u32[]{:S(2)}) %copy-start.11) | copy-done | bytes 88
  6.7 0.6 %dynamic_slice.14 = s32[1]{0:T(128)} dynamic-slice(s32[16]{0:T(128)S(1)} %copy-done.11, s32[]{:T(128)S(6)} %select_n.58), dynamic_slice_sizes={1} | dynamic-slice | bytes 12 | tf_op jit(solution)/shard_map/dynamic_slice | solution.py:84
  9.9 0.6 %copy-done.1 = s32[4]{0:T(128)S(1)} copy-done((s32[4]{0:T(128)S(1)}, s32[4]{0:T(128)}, u32[]{:S(2)}) %copy-start.1) | copy-done | bytes 40
  10.6 0.6 %dynamic_slice.15 = s32[1]{0:T(128)} dynamic-slice(s32[4]{0:T(128)S(1)} %copy-done.1, s32[]{:T(128)S(6)} %select_n.60), dynamic_slice_sizes={1} | dynamic-slice | bytes 12 | tf_op jit(solution)/shard_map/dynamic_slice | solution.py:85
  12.5 0.7 %gather_fusion = s32[16]{0:T(128)S(1)} fusion(s32[4]{0:T(128)S(1)} %copy-done.1, s32[1024]{0:T(1024)S(1)} %pad_clamp_fusion), kind=kCustom, calls=%fused_computation | custom fusion | bytes 192 | tf_op jit(solution)/shard_map/gather | solution.py:101
  14.0 0.6 %copy-done.6 = bf16[1,64,128]{2,1,0:T(8,128)(2,1)S(1)} copy-done((bf16[1,64,128]{2,1,0:T(8,128)(2,1)S(1)}, bf16[1,64,128]{2,1,0:T(8,128)(2,1)}, u32[]{:S(2)}) %copy-start.6) | copy-done | bytes 16408
  14.5 0.1 add_convert_fusion.3
  14.7 0.2 fusion.2
  14.9 0.6 %copy.13 = bf16[2,8,16,128]{3,2,1,0:T(8,128)(2,1)} copy(bf16[2,8,16,128]{3,1,2,0:T(8,128)(2,1)S(1)} %fusion.2) | data formatting | bytes 131072
  15.6 8.1 %all-to-all-start = ((bf16[16,16,128]{2,1,0:T(8,128)(2,1)}), bf16[16,16,128]{2,1,0:T(8,128)(2,1)S(1)}, u32[]{:S(2)}, u32[]{:S(2)}) async-start(bf16[16,16,128]{2,1,0:T(8,128)(2,1)} %bitcast.45), calls=%async_computation | async-start | bytes 131072 | tf_op jit(solution)/shard_map/all_to_all | solution.py:92
  23.7 6.9 %all-to-all-done = bf16[16,16,128]{2,1,0:T(8,128)(2,1)S(1)} async-done(((bf16[16,16,128]{2,1,0:T(8,128)(2,1)}), bf16[16,16,128]{2,1,0:T(8,128)(2,1)S(1)}, u32[]{:S(2)}, u32[]{:S(2)}) %all-to-all-start) | async-done | bytes 65568 | tf_op jit(solution)/shard_map/all_to_all | solution.py:92
  30.6 0.7 %copy-done.4 = bf16[128,128]{1,0:T(8,128)(2,1)S(1)} copy-done((bf16[128,128]{1,0:T(8,128)(2,1)S(1)}, bf16[128,128]{1,0:T(8,128)(2,1)}, u32[]{:S(2)}) %copy-start.4) | copy-done | bytes 32792
  31.3 0.2 fusion.60
  31.5 0.6 %copy-done.5 = bf16[128,128]{1,0:T(8,128)(2,1)S(1)} copy-done((bf16[128,128]{1,0:T(8,128)(2,1)S(1)}, bf16[128,128]{1,0:T(8,128)(2,1)}, u32[]{:S(2)}) %copy-start.5) | copy-done | bytes 32792
  32.1 0.3 multiply_reduce_fusion.2
  32.4 0.1 multiply_multiply_fusion.2
  32.7 0.9 %copy-done.9 = bf16[3,512,128]{2,1,0:T(8,128)(2,1)S(1)} copy-done((bf16[3,512,128]{2,1,0:T(8,128)(2,1)S(1)}, bf16[3,512,128]{2,1,0:T(8,128)(2,1)}, u32[]{:S(2)}) %copy-start.9) | copy-done | bytes 393240
  33.7 0.6 %multiply_reduce_fusion.1 = (f32[512]{0:T(512)S(1)}, f32[512,128]{1,0:T(8,128)S(1)}) fusion(f32[512,128]{1,0:T(8,128)S(1)} %get-tuple-element.56, bf16[3,512,128]{2,1,0:T(8,128)(2,1)S(1)} %copy-done.9, bf16[512,128]{1,0:T(8,128)(2,1)S(1)} %bitcast.129, bf16[3,128,512]{2,1,0:T(8,128)(2,1)S(1)} %copy-done.10), kind=kOutput, calls=%fused_computation.26 | convolution fusion | flops 135724544 | bytes 919552 | tf_op jit(solution)/shard_map/while/body/eval_jaxpr/dot_general | solution.py:49
  34.6 0.6 %multiply_reduce_fusion = (f32[512]{0:T(512)S(1)}, f32[512,128]{1,0:T(8,128)S(1)}) fusion(f32[512,128]{1,0:T(8,128)S(1)} %get-tuple-element.58, bf16[3,512,128]{2,1,0:T(8,128)(2,1)S(1)} %copy-done.9, bf16[512,128]{1,0:T(8,128)(2,1)S(1)} %bitcast.130, bf16[3,128,512]{2,1,0:T(8,128)(2,1)S(1)} %copy-done.10), kind=kOutput, calls=%fused_computation.23 | convolution fusion | flops 135724544 | bytes 919552 | tf_op jit(solution)/shard_map/while/body/eval_jaxpr/dot_general | solution.py:49
  35.6 0.6 %fusion.1 = bf16[512,128]{1,0:T(8,128)(2,1)S(1)} fusion(f32[512,128]{1,0:T(8,128)S(1)} %get-tuple-element.60, bf16[512,128]{1,0:T(8,128)(2,1)S(1)} %bitcast.131, bf16[3,512,128]{2,1,0:T(8,128)(2,1)S(1)} %copy-done.9, bf16[3,128,512]{2,1,0:T(8,128)(2,1)S(1)} %copy-done.10), kind=kOutput, calls=%fused_computation.9 | convolution fusion | flops 135659520 | bytes 786432 | tf_op jit(solution)/shard_map/while/body/eval_jaxpr/dot_general | solution.py:49
  36.1 0.8 %broadcast_in_dim.18 = bf16[16,64,128]{2,1,0:T(8,128)(2,1)} broadcast(bf16[]{:T(256)} %constant.86.clone.1), dimensions={} | broadcast | bytes 262146 | tf_op jit(solution)/shard_map/broadcast_in_dim | solution.py:98
  36.9 0.7 %constant_dynamic-update-slice_fusion = bf16[16,64,128]{2,1,0:T(8,128)(2,1)} fusion(bf16[16,64,128]{2,1,0:T(8,128)(2,1)} %broadcast_in_dim.18, bf16[8,64,128]{2,1,0:T(8,128)(2,1)S(1)} %bitcast.128, s32[]{:T(128)S(6)} %select_n.61), kind=kLoop, calls=%fused_computation.89 | loop fusion | bytes 262148 | tf_op jit(solution)/shard_map/dynamic_update_slice | solution.py:99
  37.5 3.5 %all-to-all-start.1 = ((bf16[16,64,128]{2,1,0:T(8,128)(2,1)}), bf16[16,64,128]{2,1,0:T(8,128)(2,1)S(1)}, u32[]{:S(2)}, u32[]{:S(2)}) async-start(bf16[16,64,128]{2,1,0:T(8,128)(2,1)} %constant_dynamic-update-slice_fusion), calls=%async_computation.1 | async-start | bytes 524288 | tf_op jit(solution)/shard_map/all_to_all | solution.py:100
  41.1 0.7 %copy-done.2 = s32[4,8]{1,0:T(4,128)S(1)} copy-done((s32[4,8]{1,0:T(4,128)S(1)}, s32[4,8]{1,0:T(4,128)}, u32[]{:S(2)}) %copy-start.2) | copy-done | bytes 152
  41.8 0.7 %gather_fusion.1 = s32[16]{0:T(128)S(1)} fusion(s32[4,8]{1,0:T(4,128)S(1)} %copy-done.2, s32[16]{0:T(128)S(1)} %fusion.47), kind=kCustom, calls=%fused_computation.1 | custom fusion | bytes 256 | tf_op jit(solution)/shard_map/gather | solution.py:104
  42.6 8.5 %all-to-all-done.1 = bf16[16,64,128]{2,1,0:T(8,128)(2,1)S(1)} async-done(((bf16[16,64,128]{2,1,0:T(8,128)(2,1)}), bf16[16,64,128]{2,1,0:T(8,128)(2,1)S(1)}, u32[]{:S(2)}, u32[]{:S(2)}) %all-to-all-start.1) | async-done | bytes 262176 | tf_op jit(solution)/shard_map/all_to_all | solution.py:100
  51.0 0.3 fusion
  51.3 0.7 %convert_element_type.88 = bf16[1,256,128]{2,1,0:T(8,128)(2,1)} reshape(bf16[4,8192]{1,0:T(4,128)(2,1)S(1)} %fusion) | data formatting | bytes 131072 | tf_op jit(solution)/shard_map/convert_element_type | solution.py:116
  (40 shorter events, 1.1 us)
Async XLA Ops:
  0.0 31.5 %copy-start = (bf16[1,8,64,128]{3,2,1,0:T(8,128)(2,1)S(1)}, bf16[1,8,64,128]{3,2,1,0:T(8,128)(2,1)}, u32[]{:S(2)}) copy-start(bf16[1,8,64,128]{3,2,1,0:T(8,128)(2,1)} %param.13) | copy-start | bytes 393220
  0.0 13.8 %collective-permute-start.1 = (bf16[1,64,128]{2,1,0:T(8,128)(2,1)}, bf16[1,64,128]{2,1,0:T(8,128)(2,1)S(1)}, u32[]{:S(2)}, u32[]{:S(2)}) collective-permute-start(bf16[1,64,128]{2,1,0:T(8,128)(2,1)} %param.12), channel_id=1, source_target_pairs={{1,0},{2,1},{3,2},{4,3},{5,4},{6,5},{7,6},{8,7},{9,8},{10,9},{11,1... | collective-permute-start | bytes 49160 | tf_op jit(solution)/shard_map/ppermute | solution.py:19
  1.4 12.5 %collective-permute-start = (bf16[1,64,128]{2,1,0:T(8,128)(2,1)}, bf16[1,64,128]{2,1,0:T(8,128)(2,1)S(1)}, u32[]{:S(2)}, u32[]{:S(2)}) collective-permute-start(bf16[1,64,128]{2,1,0:T(8,128)(2,1)} %param.12), channel_id=1, source_target_pairs={{0,1},{1,2},{2,3},{3,4},{4,5},{5,6},{6,7},{7,8},{8,9},{9,10},{10,1... | collective-permute-start | bytes 49160 | tf_op jit(solution)/shard_map/ppermute | solution.py:17
  5.1 0.9 %copy-start.7 = (f32[3,3,128]{2,1,0:T(4,128)S(1)}, f32[3,3,128]{2,1,0:T(4,128)}, u32[]{:S(2)}) copy-start(f32[3,3,128]{2,1,0:T(4,128)} %param.21) | copy-start | bytes 13828
  6.1 0.7 %copy-start.11 = (s32[16]{0:T(128)S(1)}, s32[16]{0:T(128)}, u32[]{:S(2)}) copy-start(s32[16]{0:T(128)} %param.16) | copy-start | bytes 196
  9.9 0.7 %copy-start.1 = (s32[4]{0:T(128)S(1)}, s32[4]{0:T(128)}, u32[]{:S(2)}) copy-start(s32[4]{0:T(128)} %param.14) | copy-start | bytes 52
  12.5 1.4 %copy-start.3 = (bf16[3,128,128]{2,1,0:T(8,128)(2,1)S(1)}, bf16[3,128,128]{2,1,0:T(8,128)(2,1)}, u32[]{:S(2)}) copy-start(bf16[3,128,128]{2,1,0:T(8,128)(2,1)} %param.17) | copy-start | bytes 294916
  13.8 0.7 %copy-start.6 = (bf16[1,64,128]{2,1,0:T(8,128)(2,1)S(1)}, bf16[1,64,128]{2,1,0:T(8,128)(2,1)}, u32[]{:S(2)}) copy-start(bf16[1,64,128]{2,1,0:T(8,128)(2,1)} %param.12) | copy-start | bytes 49156
  15.6 8.1 %copy-start.8 = (f32[3,128]{1,0:T(4,128)S(1)}, f32[3,128]{1,0:T(4,128)}, u32[]{:S(2)}) copy-start(f32[3,128]{1,0:T(4,128)} %param.20) | copy-start | bytes 4612
  15.6 15.0 %all-to-all-start = ((bf16[16,16,128]{2,1,0:T(8,128)(2,1)}), bf16[16,16,128]{2,1,0:T(8,128)(2,1)S(1)}, u32[]{:S(2)}, u32[]{:S(2)}) async-start(bf16[16,16,128]{2,1,0:T(8,128)(2,1)} %bitcast.45), calls=%async_computation | async-start | bytes 131072 | tf_op jit(solution)/shard_map/all_to_all | solution.py:92
  30.6 0.8 %copy-start.4 = (bf16[128,128]{1,0:T(8,128)(2,1)S(1)}, bf16[128,128]{1,0:T(8,128)(2,1)}, u32[]{:S(2)}) copy-start(bf16[128,128]{1,0:T(8,128)(2,1)} %param.18) | copy-start | bytes 98308
  31.3 0.8 %copy-start.5 = (bf16[128,128]{1,0:T(8,128)(2,1)S(1)}, bf16[128,128]{1,0:T(8,128)(2,1)}, u32[]{:S(2)}) copy-start(bf16[128,128]{1,0:T(8,128)(2,1)} %param.19) | copy-start | bytes 98308
  32.6 1.0 %copy-start.9 = (bf16[3,512,128]{2,1,0:T(8,128)(2,1)S(1)}, bf16[3,512,128]{2,1,0:T(8,128)(2,1)}, u32[]{:S(2)}) copy-start(bf16[3,512,128]{2,1,0:T(8,128)(2,1)} %param.23) | copy-start | bytes 1179652
  32.6 1.1 %copy-start.10 = (bf16[3,128,512]{2,1,0:T(8,128)(2,1)S(1)}, bf16[3,128,512]{2,1,0:T(8,128)(2,1)}, u32[]{:S(2)}) copy-start(bf16[3,128,512]{2,1,0:T(8,128)(2,1)} %param.22) | copy-start | bytes 1179652
  37.5 13.5 %all-to-all-start.1 = ((bf16[16,64,128]{2,1,0:T(8,128)(2,1)}), bf16[16,64,128]{2,1,0:T(8,128)(2,1)S(1)}, u32[]{:S(2)}, u32[]{:S(2)}) async-start(bf16[16,64,128]{2,1,0:T(8,128)(2,1)} %constant_dynamic-update-slice_fusion), calls=%async_computation.1 | async-start | bytes 524288 | tf_op jit(solution)/shard_map/all_to_all | solution.py:100
  41.1 0.7 %copy-start.2 = (s32[4,8]{1,0:T(4,128)S(1)}, s32[4,8]{1,0:T(4,128)}, u32[]{:S(2)}) copy-start(s32[4,8]{1,0:T(4,128)} %param.15) | copy-start | bytes 388
where the time goes:
time: 52.8 us; the launch traced here: 52 us
  starting transfers between devices  16.1 us (30%)
  waiting for transfers between devices  15.4 us (29%)
  local copies, waits for them, and re-layouts  10.3 us (20%)
  between operations  4.86 us (9%)
  matrix products  3.93 us (7%)
  other arithmetic  1.47 us (3%)
    all_to_all x1, waiting for transfers between devices, on_device(): lax.all_to_all(placed, 'frame', split_axis=0, concat_axis=0, tiled=True)  8.48 us
    all_to_all x1, starting transfers between devices, on_device(): lax.all_to_all(outgoing, 'frame', split_axis=0, concat_axis=0, tiled=True)  8.11 us
    all_to_all x1, waiting for transfers between devices, on_device(): lax.all_to_all(outgoing, 'frame', split_axis=0, concat_axis=0, tiled=True)  6.87 us
    unnamed x25, local copies, waits for them, and re-layouts  5.51 us
    all_to_all x1, starting transfers between devices, on_device(): lax.all_to_all(placed, 'frame', split_axis=0, concat_axis=0, tiled=True)  3.53 us
    ppermute x1, starting transfers between devices, padded_2(): lax.ppermute(tail, axis, [(i, (i + 1) % count) for i in range(ends)])  3.04 us
    dot_general x3, matrix products, refine_block(): jnp.dot(hidden, mlp_out[layer_id], preferred_element_type=jnp.float32)  1.83 us
    ppermute x1, starting transfers between devices, padded_2(): lax.ppermute(head, axis, [((i + 1) % count, i) for i in range(ends)])  1.41 us
  transfers between devices with their start and end apart: 4, of which 2 were waited for; matrix products, arithmetic and copies ran while one was open for 8% of the time, Pallas kernels for 0%

commit v1 on v0

v1 whole, which is shorter than its diff:
```python
import functools

import jax
import jax.numpy as jnp
from jax import lax
from jax.experimental import pallas as pl
from jax.experimental.pallas import tpu as pltpu
from jax.sharding import PartitionSpec as P

F32 = jnp.float32
BF16 = jnp.bfloat16
VMEM = pltpu.VMEM
SMEM = pltpu.SMEM


def dot(a, b):
    return jnp.dot(a, b, preferred_element_type=F32)


def silu(x):
    half = 0.5 * x
    return half + half * jnp.tanh(half)


def spec(space):
    return pl.BlockSpec(memory_space=space)


def pick_kernel(tiles, assign_ref, low_ref, out_ref):
    count, low_pos, _ = out_ref.shape

    def body(slot, carry):
        tile = lax.rem(assign_ref[slot], tiles)
        first = pl.multiple_of(tile * low_pos, low_pos)
        out_ref[slot] = low_ref[0, pl.ds(first, low_pos), :]
        return carry

    lax.fori_loop(0, count, body, 0, unroll=min(count, 16))


def side_kernel(
    tiles, assign_ref, starts_ref, blend_ref, noisy_ref, noise_w_ref,
    projected_ref, picker_ref, weights_ref, placed_ref,
):
    count = assign_ref.shape[0]
    windows, window_len = blend_ref.shape
    channels = noisy_ref.shape[-1]
    tile_pos = noisy_ref.shape[2]
    rows, low_rows = picker_ref.shape
    low_pos = low_rows // count
    own = lax.axis_index("frame")
    projected_ref[...] = dot(noisy_ref[0].reshape(rows, channels), noise_w_ref[...])
    start = starts_ref[assign_ref[own] // tiles]
    row = lax.broadcasted_iota(jnp.int32, (rows, low_rows), 0)
    column = lax.broadcasted_iota(jnp.int32, (rows, low_rows), 1)
    wanted = row // (tile_pos // low_pos) + start * low_pos
    picker_ref[...] = jnp.where(column == wanted, 1.0, 0.0).astype(BF16)
    placed_ref[...] = jnp.zeros_like(placed_ref)

    def factor_of(window):
        offset = own - starts_ref[window]
        inside = (offset >= 0) & (offset < window_len)
        clipped = jnp.clip(offset, 0, window_len - 1)
        return jnp.where(inside, blend_ref[window, clipped], 0)

    denom = lax.fori_loop(
        0, windows, lambda w, total: total + factor_of(w), jnp.int32(0), unroll=min(windows, 4)
    )
    denom_row = jnp.full((1, channels), denom, jnp.int32).astype(F32)
    weights_ref[...] = jnp.zeros_like(weights_ref)

    def body(slot, carry):
        item = assign_ref[slot]
        factor = factor_of(item // tiles)
        factor_row = jnp.full((1, channels), factor, jnp.int32).astype(F32)
        weights_ref[slot, pl.ds(lax.rem(item, tiles), 1), :] = factor_row / denom_row
        return carry

    lax.fori_loop(0, count, body, 0)


def refine_kernel(
    tiles, assign_hbm, starts_hbm, tile_ref, projected_ref, picker_ref, base_w_ref, cond_w_ref,
    gains_ref, tconv_ref, mlp_in_ref, mlp_out_ref, zeros_hbm, placed_hbm,
    assign_sm, starts_sm, refined_ref, sems,
):
    copies = [
        pltpu.make_async_copy(assign_hbm, assign_sm, sems.at[0]),
        pltpu.make_async_copy(starts_hbm, starts_sm, sems.at[1]),
    ]
    for copy in copies:
        copy.start()
    count, low_pos, channels = tile_ref.shape
    window_len, tile_pos, _ = refined_ref.shape
    rows = window_len * tile_pos
    frames = tile_ref[...]
    edge = jnp.zeros((1, low_pos, channels), BF16)
    before = jnp.concatenate([edge, frames[:-1]], 0).reshape(count * low_pos, channels)
    behind = jnp.concatenate([frames[1:], edge], 0).reshape(count * low_pos, channels)
    middle = frames.reshape(count * low_pos, channels)
    total = dot(before, base_w_ref[0]) + dot(middle, base_w_ref[1]) + dot(behind, base_w_ref[2])
    base = (middle.astype(F32) + silu(total)).astype(BF16)
    cond = dot(picker_ref[...], base).astype(BF16)
    state = dot(cond, cond_w_ref[...]) + projected_ref[...]
    layers = gains_ref.shape[0]
    for layer in range(layers):
        inverse = lax.rsqrt(jnp.mean(state * state, axis=-1, keepdims=True) + 1e-06)
        normed = (state * inverse * gains_ref[layer : layer + 1, :]).reshape(
            window_len, tile_pos, channels
        )
        edge = jnp.zeros((1, tile_pos, channels), F32)
        before = jnp.concatenate([edge, normed[:-1]], 0)
        behind = jnp.concatenate([normed[1:], edge], 0)
        mixed = (
            normed
            + tconv_ref[layer, 0:1, :] * before
            + tconv_ref[layer, 1:2, :] * normed
            + tconv_ref[layer, 2:3, :] * behind
        )
        mixed = mixed.reshape(rows, channels).astype(BF16)
        pieces = []
        step = rows // CHUNKS
        for piece in range(CHUNKS):
            part = slice(piece * step, (piece + 1) * step)
            hidden = silu(dot(mixed[part], mlp_in_ref[layer])).astype(BF16)
            pieces.append(state[part] + dot(hidden, mlp_out_ref[layer]))
        state = jnp.concatenate(pieces, 0) if len(pieces) > 1 else pieces[0]
    refined_ref[...] = state.astype(BF16).reshape(window_len, tile_pos, channels)
    for copy in copies:
        copy.wait()
    start = starts_sm[assign_sm[lax.axis_index("frame")] // tiles]
    out = pltpu.make_async_copy(refined_ref, placed_hbm.at[pl.ds(start, window_len)], sems.at[2])
    out.start()
    out.wait()


CHUNKS = 4


def blend_kernel(received_ref, weights_ref, video_ref):
    count, tile_pos, channels = received_ref.shape
    tiles = weights_ref.shape[1]

    def body(slot, totals):
        rows = received_ref[slot].astype(F32)
        weights = weights_ref[slot]
        return tuple(totals[t] + weights[t : t + 1, :] * rows for t in range(tiles))

    zero = jnp.zeros((tile_pos, channels), F32)
    totals = lax.fori_loop(0, count, body, (zero,) * tiles, unroll=min(count, 16))
    for t in range(tiles):
        video_ref[0, t * tile_pos : (t + 1) * tile_pos, :] = totals[t].astype(BF16)


def on_device(
    lowres, noisy, starts, blend, assign, base_w, cond_w, noise_w, gains, tconv, mlp_in, mlp_out
):
    count = assign.shape[0]
    windows, window_len = blend.shape
    tiles = count // windows
    tile_pos, channels = noisy.shape[2:]
    low_pos = lowres.shape[1] // tiles
    rows = window_len * tile_pos
    hidden = mlp_in.shape[-1]
    layers = gains.shape[0]

    outgoing = pl.pallas_call(
        functools.partial(pick_kernel, tiles),
        out_shape=jax.ShapeDtypeStruct((count, low_pos, channels), BF16),
        in_specs=[spec(SMEM), spec(VMEM)],
        out_specs=spec(VMEM),
        name="pick",
    )(assign, lowres)
    gathered = lax.all_to_all(outgoing, "frame", split_axis=0, concat_axis=0, tiled=True)

    projected, picker, weights, zeros = pl.pallas_call(
        functools.partial(side_kernel, tiles),
        out_shape=(
            jax.ShapeDtypeStruct((rows, channels), F32),
            jax.ShapeDtypeStruct((rows, count * low_pos), BF16),
            jax.ShapeDtypeStruct((count, tiles, channels), F32),
            jax.ShapeDtypeStruct((count, tile_pos, channels), BF16),
        ),
        in_specs=[spec(SMEM)] * 3 + [spec(VMEM)] * 2,
        out_specs=(spec(VMEM),) * 4,
        cost_estimate=pl.CostEstimate(
            flops=2 * rows * channels * channels, bytes_accessed=4 * rows * channels, transcendentals=0
        ),
        name="side",
    )(assign, starts, blend, noisy, noise_w)

    placed = pl.pallas_call(
        functools.partial(refine_kernel, tiles),
        out_shape=jax.ShapeDtypeStruct((count, tile_pos, channels), BF16),
        in_specs=[spec(pl.ANY)] * 2 + [spec(VMEM)] * 9 + [spec(pl.ANY)],
        out_specs=spec(pl.ANY),
        scratch_shapes=[
            SMEM(assign.shape, jnp.int32),
            SMEM(starts.shape, jnp.int32),
            VMEM((window_len, tile_pos, channels), BF16),
            pltpu.SemaphoreType.DMA((3,)),
        ],
        input_output_aliases={11: 0},
        cost_estimate=pl.CostEstimate(
            flops=4 * layers * rows * channels * hidden,
            bytes_accessed=4 * layers * channels * hidden,
            transcendentals=layers * rows * hidden,
        ),
        name="refine",
    )(
        assign, starts, gathered, projected, picker, base_w, cond_w, gains, tconv, mlp_in, mlp_out,
        zeros,
    )
    received = lax.all_to_all(placed, "frame", split_axis=0, concat_axis=0, tiled=True)
    return pl.pallas_call(
        blend_kernel,
        out_shape=jax.ShapeDtypeStruct((1, tiles * tile_pos, channels), BF16),
        in_specs=[spec(VMEM)] * 2,
        out_specs=spec(VMEM),
        name="blend",
    )(received, weights)


def solution(mesh):
    in_specs = (
        P(("groups", "frame"), None, None),
        P(("groups", "frame"), None, None, None),
        P("groups"),
        P("groups", None),
        P("groups"),
        P(),
        P(),
        P(),
        P(),
        P(),
        P(),
        P(),
    )
    out_specs = P(("groups", "frame"), None, None)
    return jax.shard_map(
        on_device, mesh=mesh, in_specs=in_specs, out_specs=out_specs, check_vma=False
    )
```

time: 52.8 us -> 37.8 us (0.72)
  blocking collectives: 0 us -> 14.2 us
  waiting for transfers between devices: 15.4 us -> 4.46 us
  Pallas kernels: 0 us -> 10.6 us
  local copies, waits for them, and re-layouts: 10.3 us -> 0.63 us
  starting transfers between devices: 16.1 us -> 7.41 us
  between operations: 4.86 us -> 0.02 us
  matrix products: 3.93 us -> 0 us
  other arithmetic: 1.47 us -> 0 us
    all_to_all x0 -> x1, blocking collectives: none -> 14.2 us  [on_device(): lax.all_to_all(placed, 'frame', split_axis=0, concat_axis=0, tiled=True)]
    pallas_call x0 -> x4, Pallas kernels: none -> 10.6 us  [the longest x1 5.06 us: on_device(): pl.pallas_call(functools.partial(refine_kernel, tiles), out_shape=jax.Sha...]
    all_to_all x1 -> x0, waiting for transfers between devices: 8.48 us -> none  [on_device(): lax.all_to_all(placed, 'frame', split_axis=0, concat_axis=0, tiled=True)]
    unnamed x25 -> x2, local copies, waits for them, and re-layouts: 5.51 us -> 0.63 us
    ppermute x2 -> x0, starting transfers between devices: 4.45 us -> none  [the longest x1 3.04 us: padded_2(): lax.ppermute(tail, axis, [(i, (i + 1) % count) for i in range(ends)])]
    dot_general x10 -> x0, matrix products: 3.93 us -> none  [the longest x3 1.83 us: refine_block(): jnp.dot(hidden, mlp_out[layer_id], preferred_element_type=jnp.float32)]
    all_to_all x1 -> x0, starting transfers between devices: 3.53 us -> none  [on_device(): lax.all_to_all(placed, 'frame', split_axis=0, concat_axis=0, tiled=True)]
    all_to_all x1, waiting for transfers between devices: 6.87 us -> 4.46 us  [on_device(): lax.all_to_all(outgoing, 'frame', split_axis=0, concat_axis=0, tiled=True)]
  transfers between devices with their start and end apart: 4 -> 1, of which waited for: 2 -> 1; matrix products, arithmetic and copies ran while one was open for 8% -> 0% of each run, Pallas kernels for 0% -> 7%
where the time goes in v1:
time: 37.8 us; the launch traced here: 37.4 us
  blocking collectives  14.2 us (38%)
  Pallas kernels  10.6 us (28%)
  starting transfers between devices  7.41 us (20%)
  waiting for transfers between devices  4.46 us (12%)
  local copies, waits for them, and re-layouts  0.63 us (2%)
    all_to_all x1, blocking collectives, on_device(): lax.all_to_all(placed, 'frame', split_axis=0, concat_axis=0, tiled=True)  14.2 us
    all_to_all x1, starting transfers between devices, on_device(): lax.all_to_all(outgoing, 'frame', split_axis=0, concat_axis=0, tiled=True)  7.41 us
    pallas_call x1, Pallas kernels, on_device(): pl.pallas_call(functools.partial(refine_kernel, tiles), out_shape=jax.Sha...  5.06 us
    all_to_all x1, waiting for transfers between devices, on_device(): lax.all_to_all(outgoing, 'frame', split_axis=0, concat_axis=0, tiled=True)  4.46 us
    pallas_call x1, Pallas kernels, on_device(): pl.pallas_call(functools.partial(side_kernel, tiles), out_shape=(jax.Shap...  2.43 us
    pallas_call x1, Pallas kernels, on_device(): pl.pallas_call(blend_kernel, out_shape=jax.ShapeDtypeStruct((1, tiles * t...  1.74 us
    pallas_call x1, Pallas kernels, on_device(): pl.pallas_call(functools.partial(pick_kernel, tiles), out_shape=jax.Shape...  1.4 us
  transfers between devices with their start and end apart: 1, of which 1 were waited for; matrix products, arithmetic and copies ran while one was open for 0% of the time, Pallas kernels for 7%

profile of v1, /device:TPU:0, one launch (start us, length us, event | category | flops | bytes accessed | tf_op | source)
XLA Modules:
  0.0 37.4 jit_solution(3875055247874403808)
XLA Ops:
  0.0 1.4 %pick.1 = bf16[16,16,128]{2,1,0:T(8,128)(2,1)} custom-call(s32[16]{0:T(128)} %assign_hbm.1, bf16[1,64,128]{2,1,0:T(8,128)(2,1)} %low_ref.1), custom_call_target="tpu_custom_call" | custom-call | tf_op jit(solution)/shard_map/pick/pallas_call | solution.py:167
  1.4 7.4 %all-to-all-start = ((bf16[16,16,128]{2,1,0:T(8,128)(2,1)}), bf16[16,16,128]{2,1,0:T(8,128)(2,1)S(1)}, u32[]{:S(2)}, u32[]{:S(2)}) async-start(bf16[16,16,128]{2,1,0:T(8,128)(2,1)} %pick.1), calls=%async_computation | async-start | bytes 131072 | tf_op jit(solution)/shard_map/all_to_all | solution.py:174
  8.8 2.4 %side.1 = (f32[512,128]{1,0:T(8,128)}, bf16[512,256]{1,0:T(8,128)(2,1)}, f32[16,4,128]{2,1,0:T(4,128)}, bf16[16,64,128]{2,1,0:T(8,128)(2,1)}) custom-call(s32[16]{0:T(128)} %assign_hbm.1, s32[4]{0:T(128)} %starts_hbm.1, s32[4,8]{1,0:T(4,128)} %blend_ref.1, bf16[1,8,64,128]{3,2,1,0:T(8,128)(2,1)} %noisy_ref.1, bf16[128,128]{1,0:T(8,128)(2,1)} %noise_w_ref.1), custom_call_target="tpu_custom_call" | custom-call | flops 16777216 | bytes 262144 | tf_op jit(solution)/shard_map/side/pallas_call | solution.py:176
  11.3 4.5 %all-to-all-done.tile_ref = bf16[16,16,128]{2,1,0:T(8,128)(2,1)S(1)} async-done(((bf16[16,16,128]{2,1,0:T(8,128)(2,1)}), bf16[16,16,128]{2,1,0:T(8,128)(2,1)S(1)}, u32[]{:S(2)}, u32[]{:S(2)}) %all-to-all-start) | async-done | bytes 65568 | tf_op jit(solution)/shard_map/all_to_all | solution.py:174
  15.7 0.0 copy-start
  15.7 0.6 %copy-done = bf16[16,16,128]{2,1,0:T(8,128)(2,1)} copy-done((bf16[16,16,128]{2,1,0:T(8,128)(2,1)}, bf16[16,16,128]{2,1,0:T(8,128)(2,1)S(1)}, u32[]{:S(2)}) %copy-start) | copy-done | bytes 65560
  16.4 5.1 %refine.1 = bf16[16,64,128]{2,1,0:T(8,128)(2,1)} custom-call(s32[16]{0:T(128)} %assign_hbm.1, s32[4]{0:T(128)} %starts_hbm.1, bf16[16,16,128]{2,1,0:T(8,128)(2,1)} %copy-done, f32[512,128]{1,0:T(8,128)} %get-tuple-element.9.projected_ref, bf16[512,256]{1,0:T(8,128)(2,1)} %get-tuple-element.10.picker_ref, ...), custom_call_target="tpu_custom_call", output_to_operand_aliasing={{}: (11, {})} | custom-call | flops 402653184 | bytes 786432 | tf_op jit(solution)/shard_map/refine/pallas_call | solution.py:192
  21.4 14.2 %all_to_all.10.received_ref = bf16[16,64,128]{2,1,0:T(8,128)(2,1)} all-to-all(bf16[16,64,128]{2,1,0:T(8,128)(2,1)} %refine.1), channel_id=1, replica_groups=mesh['groups'=2,'frame'=16] {'frame'}, dimensions={0} | all-to-all | bytes 524288 | tf_op jit(solution)/shard_map/all_to_all | solution.py:214
  35.6 1.7 %blend.1 = bf16[1,256,128]{2,1,0:T(8,128)(2,1)} custom-call(bf16[16,64,128]{2,1,0:T(8,128)(2,1)} %all_to_all.10.received_ref, f32[16,4,128]{2,1,0:T(4,128)} %get-tuple-element.12.weights_ref), custom_call_target="tpu_custom_call" | custom-call | tf_op jit(solution)/shard_map/blend/pallas_call | solution.py:215
Async XLA Ops:
  1.4 14.3 %all-to-all-start = ((bf16[16,16,128]{2,1,0:T(8,128)(2,1)}), bf16[16,16,128]{2,1,0:T(8,128)(2,1)S(1)}, u32[]{:S(2)}, u32[]{:S(2)}) async-start(bf16[16,16,128]{2,1,0:T(8,128)(2,1)} %pick.1), calls=%async_computation | async-start | bytes 131072 | tf_op jit(solution)/shard_map/all_to_all | solution.py:174
  15.7 0.6 %copy-start = (bf16[16,16,128]{2,1,0:T(8,128)(2,1)}, bf16[16,16,128]{2,1,0:T(8,128)(2,1)S(1)}, u32[]{:S(2)}) copy-start(bf16[16,16,128]{2,1,0:T(8,128)(2,1)S(1)} %all-to-all-done.tile_ref) | copy-start | bytes 196612

commit v2 on v1

--- a/solution.py
+++ b/solution.py
@@ -11,6 +11,7 @@
 BF16 = jnp.bfloat16
 VMEM = pltpu.VMEM
 SMEM = pltpu.SMEM
+ROOM = 24 << 20
 
 
 def dot(a, b):
@@ -24,6 +25,14 @@
 
 def spec(space):
     return pl.BlockSpec(memory_space=space)
+
+
+def near(*arrays):
+    return tuple(pltpu.with_memory_space_constraint(array, VMEM) for array in arrays)
+
+
+def far(*arrays):
+    return tuple(pltpu.with_memory_space_constraint(array, pltpu.HBM) for array in arrays)
 
 
 def pick_kernel(tiles, assign_ref, low_ref, out_ref):
@@ -39,9 +48,17 @@
 
 
 def side_kernel(
-    tiles, assign_ref, starts_ref, blend_ref, noisy_ref, noise_w_ref,
-    projected_ref, picker_ref, weights_ref, placed_ref,
+    tiles, assign_ref, starts_ref, blend_ref, noisy_ref, noise_w_ref, *refs
 ):
+    moved = (len(refs) - 5) // 2
+    sources, targets, sems = refs[:moved], refs[moved + 4 : -1], refs[-1]
+    projected_ref, picker_ref, weights_ref, placed_ref = refs[moved : moved + 4]
+    copies = [
+        pltpu.make_async_copy(source, target, sems.at[k])
+        for k, (source, target) in enumerate(zip(sources, targets))
+    ]
+    for copy in copies:
+        copy.start()
     count = assign_ref.shape[0]
     windows, window_len = blend_ref.shape
     channels = noisy_ref.shape[-1]
@@ -77,12 +94,14 @@
         return carry
 
     lax.fori_loop(0, count, body, 0)
+    for copy in copies:
+        copy.wait()
 
 
 def refine_kernel(
     tiles, assign_hbm, starts_hbm, tile_ref, projected_ref, picker_ref, base_w_ref, cond_w_ref,
-    gains_ref, tconv_ref, mlp_in_ref, mlp_out_ref, zeros_hbm, placed_hbm,
-    assign_sm, starts_sm, refined_ref, sems,
+    gains_ref, tconv_ref, mlp_in_ref, mlp_out_ref, zeros_ref, placed_ref,
+    assign_sm, starts_sm, sems,
 ):
     copies = [
         pltpu.make_async_copy(assign_hbm, assign_sm, sems.at[0]),
@@ -91,8 +110,9 @@
     for copy in copies:
         copy.start()
     count, low_pos, channels = tile_ref.shape
-    window_len, tile_pos, _ = refined_ref.shape
-    rows = window_len * tile_pos
+    rows = projected_ref.shape[0]
+    tile_pos = placed_ref.shape[1]
+    window_len = rows // tile_pos
     frames = tile_ref[...]
     edge = jnp.zeros((1, low_pos, channels), BF16)
     before = jnp.concatenate([edge, frames[:-1]], 0).reshape(count * low_pos, channels)
@@ -125,13 +145,12 @@
             hidden = silu(dot(mixed[part], mlp_in_ref[layer])).astype(BF16)
             pieces.append(state[part] + dot(hidden, mlp_out_ref[layer]))
         state = jnp.concatenate(pieces, 0) if len(pieces) > 1 else pieces[0]
-    refined_ref[...] = state.astype(BF16).reshape(window_len, tile_pos, channels)
     for copy in copies:
         copy.wait()
     start = starts_sm[assign_sm[lax.axis_index("frame")] // tiles]
-    out = pltpu.make_async_copy(refined_ref, placed_hbm.at[pl.ds(start, window_len)], sems.at[2])
-    out.start()
-    out.wait()
+    placed_ref[pl.ds(start, window_len)] = state.astype(BF16).reshape(
+        window_len, tile_pos, channels
+    )
 
 
 CHUNKS = 4
@@ -166,39 +185,43 @@
 
     outgoing = pl.pallas_call(
         functools.partial(pick_kernel, tiles),
-        out_shape=jax.ShapeDtypeStruct((count, low_pos, channels), BF16),
+        out_shape=VMEM((count, low_pos, channels), BF16),
         in_specs=[spec(SMEM), spec(VMEM)],
         out_specs=spec(VMEM),
+        compiler_params=pltpu.CompilerParams(vmem_limit_bytes=ROOM),
         name="pick",
-    )(assign, lowres)
+    )(*far(assign, lowres))
     gathered = lax.all_to_all(outgoing, "frame", split_axis=0, concat_axis=0, tiled=True)
 
-    projected, picker, weights, zeros = pl.pallas_call(
+    moved = (base_w, cond_w, gains, tconv, mlp_in, mlp_out)
+    projected, picker, weights, zeros, *params = pl.pallas_call(
         functools.partial(side_kernel, tiles),
         out_shape=(
-            jax.ShapeDtypeStruct((rows, channels), F32),
-            jax.ShapeDtypeStruct((rows, count * low_pos), BF16),
-            jax.ShapeDtypeStruct((count, tiles, channels), F32),
-            jax.ShapeDtypeStruct((count, tile_pos, channels), BF16),
+            VMEM((rows, channels), F32),
+            VMEM((rows, count * low_pos), BF16),
+            VMEM((count, tiles, channels), F32),
+            VMEM((count, tile_pos, channels), BF16),
+            *(VMEM(array.shape, array.dtype) for array in moved),
         ),
-        in_specs=[spec(SMEM)] * 3 + [spec(VMEM)] * 2,
-        out_specs=(spec(VMEM),) * 4,
+        in_specs=[spec(SMEM)] * 3 + [spec(VMEM)] * 2 + [spec(pl.ANY)] * len(moved),
+        out_specs=(spec(VMEM),) * (4 + len(moved)),
+        scratch_shapes=[pltpu.SemaphoreType.DMA((len(moved),))],
         cost_estimate=pl.CostEstimate(
             flops=2 * rows * channels * channels, bytes_accessed=4 * rows * channels, transcendentals=0
         ),
+        compiler_params=pltpu.CompilerParams(vmem_limit_bytes=ROOM),
         name="side",
-    )(assign, starts, blend, noisy, noise_w)
+    )(*far(assign, starts, blend, noisy, noise_w, *moved))
 
     placed = pl.pallas_call(
         functools.partial(refine_kernel, tiles),
-        out_shape=jax.ShapeDtypeStruct((count, tile_pos, channels), BF16),
-        in_specs=[spec(pl.ANY)] * 2 + [spec(VMEM)] * 9 + [spec(pl.ANY)],
-        out_specs=spec(pl.ANY),
+        out_shape=VMEM((count, tile_pos, channels), BF16),
+        in_specs=[spec(pl.ANY)] * 2 + [spec(VMEM)] * 10,
+        out_specs=spec(VMEM),
         scratch_shapes=[
             SMEM(assign.shape, jnp.int32),
             SMEM(starts.shape, jnp.int32),
-            VMEM((window_len, tile_pos, channels), BF16),
-            pltpu.SemaphoreType.DMA((3,)),
+            pltpu.SemaphoreType.DMA((2,)),
         ],
         input_output_aliases={11: 0},
         cost_estimate=pl.CostEstimate(
@@ -206,10 +229,11 @@
             bytes_accessed=4 * layers * channels * hidden,
             transcendentals=layers * rows * hidden,
         ),
+        compiler_params=pltpu.CompilerParams(vmem_limit_bytes=ROOM),
         name="refine",
     )(
-        assign, starts, gathered, projected, picker, base_w, cond_w, gains, tconv, mlp_in, mlp_out,
-        zeros,
+        *far(assign, starts),
+        *near(gathered, projected, picker, *params, zeros),
     )
     received = lax.all_to_all(placed, "frame", split_axis=0, concat_axis=0, tiled=True)
     return pl.pallas_call(
@@ -217,8 +241,9 @@
         out_shape=jax.ShapeDtypeStruct((1, tiles * tile_pos, channels), BF16),
         in_specs=[spec(VMEM)] * 2,
         out_specs=spec(VMEM),
+        compiler_params=pltpu.CompilerParams(vmem_limit_bytes=ROOM),
         name="blend",
-    )(received, weights)
+    )(*near(received, weights))
 
 
 def solution(mesh):

time: 37.8 us -> 32.9 us (0.87)
  Pallas kernels: 10.6 us -> 7.81 us
  blocking collectives: 14.2 us -> 12.6 us
  local copies, waits for them, and re-layouts: 0.63 us -> 0 us
    pallas_call x3, Pallas kernels: 8.9 us -> 7.03 us  [the longest x1 3.39 us: on_device(): pl.pallas_call(functools.partial(refine_kernel, tiles), out_shape=VMEM((c...]
    all_to_all x1, blocking collectives: 14.2 us -> 12.6 us  [on_device(): lax.all_to_all(placed, 'frame', split_axis=0, concat_axis=0, tiled=True)]
    pallas_call x1, Pallas kernels: 1.74 us -> 0.79 us  [on_device(): pl.pallas_call(blend_kernel, out_shape=jax.ShapeDtypeStruct((1, tiles * t...]
    unnamed x2 -> x0, local copies, waits for them, and re-layouts: 0.63 us -> none
where the time goes in v2:
time: 32.9 us; the launch traced here: 32.5 us
  blocking collectives  12.6 us (38%)
  Pallas kernels  7.81 us (24%)
  starting transfers between devices  7.41 us (23%)
  waiting for transfers between devices  4.66 us (14%)
    all_to_all x1, blocking collectives, on_device(): lax.all_to_all(placed, 'frame', split_axis=0, concat_axis=0, tiled=True)  12.6 us
    all_to_all x1, starting transfers between devices, on_device(): lax.all_to_all(outgoing, 'frame', split_axis=0, concat_axis=0, tiled=True)  7.41 us
    all_to_all x1, waiting for transfers between devices, on_device(): lax.all_to_all(outgoing, 'frame', split_axis=0, concat_axis=0, tiled=True)  4.66 us
    pallas_call x1, Pallas kernels, on_device(): pl.pallas_call(functools.partial(refine_kernel, tiles), out_shape=VMEM((c...  3.39 us
    pallas_call x1, Pallas kernels, on_device(): pl.pallas_call(functools.partial(side_kernel, tiles), out_shape=(VMEM((ro...  2.23 us
    pallas_call x1, Pallas kernels, on_device(): pl.pallas_call(functools.partial(pick_kernel, tiles), out_shape=VMEM((cou...  1.4 us
    pallas_call x1, Pallas kernels, on_device(): pl.pallas_call(blend_kernel, out_shape=jax.ShapeDtypeStruct((1, tiles * t...  0.79 us
  transfers between devices with their start and end apart: 1, of which 1 were waited for; matrix products, arithmetic and copies ran while one was open for 0% of the time, Pallas kernels for 7%

profile of v2, /device:TPU:0, one launch (start us, length us, event | category | flops | bytes accessed | tf_op | source)
XLA Modules:
  0.0 32.5 jit_solution(17238896963483273896)
XLA Ops:
  0.0 1.4 %pick.1 = bf16[16,16,128]{2,1,0:T(8,128)(2,1)} custom-call(s32[16]{0:T(128)} %assign_hbm.1, bf16[1,64,128]{2,1,0:T(8,128)(2,1)} %low_ref.1), custom_call_target="tpu_custom_call" | custom-call | tf_op jit(solution)/shard_map/pick/pallas_call | solution.py:186
  1.4 7.4 %all-to-all-start = ((bf16[16,16,128]{2,1,0:T(8,128)(2,1)}), bf16[16,16,128]{2,1,0:T(8,128)(2,1)S(1)}, u32[]{:S(2)}, u32[]{:S(2)}) async-start(bf16[16,16,128]{2,1,0:T(8,128)(2,1)} %pick.1), calls=%async_computation | async-start | bytes 131072 | tf_op jit(solution)/shard_map/all_to_all | solution.py:194
  8.8 2.2 %side.1 = (f32[512,128]{1,0:T(8,128)S(1)}, bf16[512,256]{1,0:T(8,128)(2,1)S(1)}, f32[16,4,128]{2,1,0:T(4,128)S(1)}, bf16[16,64,128]{2,1,0:T(8,128)(2,1)S(1)}, bf...) custom-call(s32[16]{0:T(128)} %assign_hbm.1, ...), custom_call_target="tpu_custom_call" | custom-call | flops 16777216 | bytes 262144 | tf_op jit(solution)/shard_map/side/pallas_call | solution.py:197
  11.1 4.7 %all-to-all-done.tile_ref = bf16[16,16,128]{2,1,0:T(8,128)(2,1)S(1)} async-done(((bf16[16,16,128]{2,1,0:T(8,128)(2,1)}), bf16[16,16,128]{2,1,0:T(8,128)(2,1)S(1)}, u32[]{:S(2)}, u32[]{:S(2)}) %all-to-all-start) | async-done | bytes 65568 | tf_op jit(solution)/shard_map/all_to_all | solution.py:194
  15.7 3.4 %refine.1 = bf16[16,64,128]{2,1,0:T(8,128)(2,1)S(1)} custom-call(s32[16]{0:T(128)} %assign_hbm.1, s32[4]{0:T(128)} %starts_hbm.1, bf16[16,16,128]{2,1,0:T(8,128)(2,1)S(1)} %all-to-all-done.tile_ref, f32[512,128]{1,0:T(8,128)S(1)} %get-tuple-element.15.projected_ref, ...), custom_call_target="tpu_custom_call", output_to_operand_aliasing={{}: (11, {})} | custom-call | flops 402653184 | bytes 786432 | tf_op jit(solution)/shard_map/refine/pallas_call | solution.py:216
  19.1 12.6 %all_to_all.10.received_ref = bf16[16,64,128]{2,1,0:T(8,128)(2,1)S(1)} all-to-all(bf16[16,64,128]{2,1,0:T(8,128)(2,1)S(1)} %refine.1), channel_id=1, replica_groups=mesh['groups'=2,'frame'=16] {'frame'}, dimensions={0} | all-to-all | bytes 524288 | tf_op jit(solution)/shard_map/all_to_all | solution.py:238
  31.7 0.8 %blend.1 = bf16[1,256,128]{2,1,0:T(8,128)(2,1)} custom-call(bf16[16,64,128]{2,1,0:T(8,128)(2,1)S(1)} %all_to_all.10.received_ref, f32[16,4,128]{2,1,0:T(4,128)S(1)} %get-tuple-element.24.weights_ref), custom_call_target="tpu_custom_call" | custom-call | tf_op jit(solution)/shard_map/blend/pallas_call | solution.py:239
Async XLA Ops:
  1.4 14.3 %all-to-all-start = ((bf16[16,16,128]{2,1,0:T(8,128)(2,1)}), bf16[16,16,128]{2,1,0:T(8,128)(2,1)S(1)}, u32[]{:S(2)}, u32[]{:S(2)}) async-start(bf16[16,16,128]{2,1,0:T(8,128)(2,1)} %pick.1), calls=%async_computation | async-start | bytes 131072 | tf_op jit(solution)/shard_map/all_to_all | solution.py:194

commit v3 on v2

--- a/solution.py
+++ b/solution.py
@@ -35,13 +35,25 @@
     return tuple(pltpu.with_memory_space_constraint(array, pltpu.HBM) for array in arrays)
 
 
+def rank_of(frame, count):
+    return lax.rem(frame + count // 2, jnp.int32(count))
+
+
+def exchange(blocks):
+    count = blocks.shape[0]
+    order = [(rank + count // 2) % count for rank in range(count)]
+    return lax.all_to_all(
+        blocks, "frame", split_axis=0, concat_axis=0, tiled=True, axis_index_groups=[order]
+    )
+
+
 def pick_kernel(tiles, assign_ref, low_ref, out_ref):
     count, low_pos, _ = out_ref.shape
 
     def body(slot, carry):
         tile = lax.rem(assign_ref[slot], tiles)
         first = pl.multiple_of(tile * low_pos, low_pos)
-        out_ref[slot] = low_ref[0, pl.ds(first, low_pos), :]
+        out_ref[rank_of(slot, count)] = low_ref[0, pl.ds(first, low_pos), :]
         return carry
 
     lax.fori_loop(0, count, body, 0, unroll=min(count, 16))
@@ -90,7 +102,7 @@
         item = assign_ref[slot]
         factor = factor_of(item // tiles)
         factor_row = jnp.full((1, channels), factor, jnp.int32).astype(F32)
-        weights_ref[slot, pl.ds(lax.rem(item, tiles), 1), :] = factor_row / denom_row
+        weights_ref[rank_of(slot, count), pl.ds(lax.rem(item, tiles), 1), :] = factor_row / denom_row
         return carry
 
     lax.fori_loop(0, count, body, 0)
@@ -113,7 +125,8 @@
     rows = projected_ref.shape[0]
     tile_pos = placed_ref.shape[1]
     window_len = rows // tile_pos
-    frames = tile_ref[...]
+    half = count // 2
+    frames = jnp.concatenate([tile_ref[half:], tile_ref[:half]], 0)
     edge = jnp.zeros((1, low_pos, channels), BF16)
     before = jnp.concatenate([edge, frames[:-1]], 0).reshape(count * low_pos, channels)
     behind = jnp.concatenate([frames[1:], edge], 0).reshape(count * low_pos, channels)
@@ -148,9 +161,9 @@
     for copy in copies:
         copy.wait()
     start = starts_sm[assign_sm[lax.axis_index("frame")] // tiles]
-    placed_ref[pl.ds(start, window_len)] = state.astype(BF16).reshape(
-        window_len, tile_pos, channels
-    )
+    refined = state.astype(BF16).reshape(window_len, tile_pos, channels)
+    for frame in range(window_len):
+        placed_ref[rank_of(start + frame, count)] = refined[frame]
 
 
 CHUNKS = 4
@@ -191,7 +204,7 @@
         compiler_params=pltpu.CompilerParams(vmem_limit_bytes=ROOM),
         name="pick",
     )(*far(assign, lowres))
-    gathered = lax.all_to_all(outgoing, "frame", split_axis=0, concat_axis=0, tiled=True)
+    gathered = exchange(outgoing)
 
     moved = (base_w, cond_w, gains, tconv, mlp_in, mlp_out)
     projected, picker, weights, zeros, *params = pl.pallas_call(
@@ -235,7 +248,7 @@
         *far(assign, starts),
         *near(gathered, projected, picker, *params, zeros),
     )
-    received = lax.all_to_all(placed, "frame", split_axis=0, concat_axis=0, tiled=True)
+    received = exchange(placed)
     return pl.pallas_call(
         blend_kernel,
         out_shape=jax.ShapeDtypeStruct((1, tiles * tile_pos, channels), BF16),

time: 32.9 us -> 30.2 us (0.918)
  waiting for transfers between devices: 4.66 us -> 2.41 us
  blocking collectives: 12.6 us -> 11.8 us
  starting transfers between devices: 7.41 us -> 7.89 us
    all_to_all x1, waiting for transfers between devices: 4.66 us -> 2.41 us  [exchange(): lax.all_to_all(blocks, 'frame', split_axis=0, concat_axis=0, tiled=True,...]
    all_to_all x1, blocking collectives: 12.6 us -> 11.8 us  [exchange(): lax.all_to_all(blocks, 'frame', split_axis=0, concat_axis=0, tiled=True,...]
    all_to_all x1, starting transfers between devices: 7.41 us -> 7.89 us  [exchange(): lax.all_to_all(blocks, 'frame', split_axis=0, concat_axis=0, tiled=True,...]
where the time goes in v3:
time: 30.2 us; the launch traced here: 29.9 us
  blocking collectives  11.8 us (39%)
  starting transfers between devices  7.89 us (26%)
  Pallas kernels  7.81 us (26%)
  waiting for transfers between devices  2.41 us (8%)
    all_to_all x1, blocking collectives, exchange(): lax.all_to_all(blocks, 'frame', split_axis=0, concat_axis=0, tiled=True,...  11.8 us
    all_to_all x1, starting transfers between devices, exchange(): lax.all_to_all(blocks, 'frame', split_axis=0, concat_axis=0, tiled=True,...  7.89 us
    pallas_call x1, Pallas kernels, on_device(): pl.pallas_call(functools.partial(refine_kernel, tiles), out_shape=VMEM((c...  3.4 us
    all_to_all x1, waiting for transfers between devices, exchange(): lax.all_to_all(blocks, 'frame', split_axis=0, concat_axis=0, tiled=True,...  2.41 us
    pallas_call x1, Pallas kernels, on_device(): pl.pallas_call(functools.partial(side_kernel, tiles), out_shape=(VMEM((ro...  2.21 us
    pallas_call x1, Pallas kernels, on_device(): pl.pallas_call(functools.partial(pick_kernel, tiles), out_shape=VMEM((cou...  1.4 us
    pallas_call x1, Pallas kernels, on_device(): pl.pallas_call(blend_kernel, out_shape=jax.ShapeDtypeStruct((1, tiles * t...  0.79 us
  transfers between devices with their start and end apart: 1, of which 1 were waited for; matrix products, arithmetic and copies ran while one was open for 0% of the time, Pallas kernels for 7%

profile of v3, /device:TPU:0, one launch (start us, length us, event | category | flops | bytes accessed | tf_op | source)
XLA Modules:
  0.0 29.9 jit_solution(17119483784463696024)
XLA Ops:
  0.0 1.4 %pick.1 = bf16[16,16,128]{2,1,0:T(8,128)(2,1)} custom-call(s32[16]{0:T(128)} %assign_hbm.1, bf16[1,64,128]{2,1,0:T(8,128)(2,1)} %low_ref.1), custom_call_target="tpu_custom_call" | custom-call | tf_op jit(solution)/shard_map/pick/pallas_call | solution.py:199
  1.4 7.9 %all-to-all-start = ((bf16[16,16,128]{2,1,0:T(8,128)(2,1)}), bf16[16,16,128]{2,1,0:T(8,128)(2,1)S(1)}, u32[]{:S(2)}, u32[]{:S(2)}) async-start(bf16[16,16,128]{2,1,0:T(8,128)(2,1)} %pick.1), calls=%async_computation | async-start | bytes 131072 | tf_op jit(solution)/shard_map/all_to_all | solution.py:45
  9.3 2.2 %side.1 = (f32[512,128]{1,0:T(8,128)S(1)}, bf16[512,256]{1,0:T(8,128)(2,1)S(1)}, f32[16,4,128]{2,1,0:T(4,128)S(1)}, bf16[16,64,128]{2,1,0:T(8,128)(2,1)S(1)}, bf...) custom-call(s32[16]{0:T(128)} %assign_hbm.1, ...), custom_call_target="tpu_custom_call" | custom-call | flops 16777216 | bytes 262144 | tf_op jit(solution)/shard_map/side/pallas_call | solution.py:210
  11.5 2.4 %all-to-all-done.tile_ref = bf16[16,16,128]{2,1,0:T(8,128)(2,1)S(1)} async-done(((bf16[16,16,128]{2,1,0:T(8,128)(2,1)}), bf16[16,16,128]{2,1,0:T(8,128)(2,1)S(1)}, u32[]{:S(2)}, u32[]{:S(2)}) %all-to-all-start) | async-done | bytes 65568 | tf_op jit(solution)/shard_map/all_to_all | solution.py:45
  13.9 3.4 %refine.1 = bf16[16,64,128]{2,1,0:T(8,128)(2,1)S(1)} custom-call(s32[16]{0:T(128)} %assign_hbm.1, s32[4]{0:T(128)} %starts_hbm.1, bf16[16,16,128]{2,1,0:T(8,128)(2,1)S(1)} %all-to-all-done.tile_ref, f32[512,128]{1,0:T(8,128)S(1)} %get-tuple-element.15.projected_ref, ...), custom_call_target="tpu_custom_call", output_to_operand_aliasing={{}: (11, {})} | custom-call | flops 402653184 | bytes 786432 | tf_op jit(solution)/shard_map/refine/pallas_call | solution.py:229
  17.3 11.8 %all_to_all.10.received_ref = bf16[16,64,128]{2,1,0:T(8,128)(2,1)S(1)} all-to-all(bf16[16,64,128]{2,1,0:T(8,128)(2,1)S(1)} %refine.1), channel_id=1, replica_groups={{8,9,10,11,12,13,14,15,0,1,2,3,4,5,6,7},{24,25,26,27,28,29,30,31,16,17,..., dimensions={0} | all-to-all | bytes 524288 | tf_op jit(solution)/shard_map/all_to_all | solution.py:45
  29.1 0.8 %blend.1 = bf16[1,256,128]{2,1,0:T(8,128)(2,1)} custom-call(bf16[16,64,128]{2,1,0:T(8,128)(2,1)S(1)} %all_to_all.10.received_ref, f32[16,4,128]{2,1,0:T(4,128)S(1)} %get-tuple-element.24.weights_ref), custom_call_target="tpu_custom_call" | custom-call | tf_op jit(solution)/shard_map/blend/pallas_call | solution.py:252
Async XLA Ops:
  1.4 12.5 %all-to-all-start = ((bf16[16,16,128]{2,1,0:T(8,128)(2,1)}), bf16[16,16,128]{2,1,0:T(8,128)(2,1)S(1)}, u32[]{:S(2)}, u32[]{:S(2)}) async-start(bf16[16,16,128]{2,1,0:T(8,128)(2,1)} %pick.1), calls=%async_computation | async-start | bytes 131072 | tf_op jit(solution)/shard_map/all_to_all | solution.py:45

commit v4 on v3

--- a/solution.py
+++ b/solution.py
@@ -64,7 +64,7 @@
 ):
     moved = (len(refs) - 5) // 2
     sources, targets, sems = refs[:moved], refs[moved + 4 : -1], refs[-1]
-    projected_ref, picker_ref, weights_ref, placed_ref = refs[moved : moved + 4]
+    projected_ref, weights_ref, placed_ref, start_ref = refs[moved : moved + 4]
     copies = [
         pltpu.make_async_copy(source, target, sems.at[k])
         for k, (source, target) in enumerate(zip(sources, targets))
@@ -75,15 +75,10 @@
     windows, window_len = blend_ref.shape
     channels = noisy_ref.shape[-1]
     tile_pos = noisy_ref.shape[2]
-    rows, low_rows = picker_ref.shape
-    low_pos = low_rows // count
+    rows = projected_ref.shape[0]
     own = lax.axis_index("frame")
     projected_ref[...] = dot(noisy_ref[0].reshape(rows, channels), noise_w_ref[...])
-    start = starts_ref[assign_ref[own] // tiles]
-    row = lax.broadcasted_iota(jnp.int32, (rows, low_rows), 0)
-    column = lax.broadcasted_iota(jnp.int32, (rows, low_rows), 1)
-    wanted = row // (tile_pos // low_pos) + start * low_pos
-    picker_ref[...] = jnp.where(column == wanted, 1.0, 0.0).astype(BF16)
+    start_ref[0] = starts_ref[assign_ref[own] // tiles]
     placed_ref[...] = jnp.zeros_like(placed_ref)
 
     def factor_of(window):
@@ -111,62 +106,57 @@
 
 
 def refine_kernel(
-    tiles, assign_hbm, starts_hbm, tile_ref, projected_ref, picker_ref, base_w_ref, cond_w_ref,
-    gains_ref, tconv_ref, mlp_in_ref, mlp_out_ref, zeros_ref, placed_ref,
-    assign_sm, starts_sm, sems,
+    start_ref, tile_ref, projected_ref, base_w_ref, cond_w_ref, gains_ref, tconv_ref, mlp_in_ref,
+    mlp_out_ref, zeros_ref, placed_ref, state_ref,
 ):
-    copies = [
-        pltpu.make_async_copy(assign_hbm, assign_sm, sems.at[0]),
-        pltpu.make_async_copy(starts_hbm, starts_sm, sems.at[1]),
-    ]
-    for copy in copies:
-        copy.start()
     count, low_pos, channels = tile_ref.shape
     rows = projected_ref.shape[0]
     tile_pos = placed_ref.shape[1]
     window_len = rows // tile_pos
-    half = count // 2
-    frames = jnp.concatenate([tile_ref[half:], tile_ref[:half]], 0)
-    edge = jnp.zeros((1, low_pos, channels), BF16)
-    before = jnp.concatenate([edge, frames[:-1]], 0).reshape(count * low_pos, channels)
-    behind = jnp.concatenate([frames[1:], edge], 0).reshape(count * low_pos, channels)
-    middle = frames.reshape(count * low_pos, channels)
-    total = dot(before, base_w_ref[0]) + dot(middle, base_w_ref[1]) + dot(behind, base_w_ref[2])
-    base = (middle.astype(F32) + silu(total)).astype(BF16)
-    cond = dot(picker_ref[...], base).astype(BF16)
-    state = dot(cond, cond_w_ref[...]) + projected_ref[...]
-    layers = gains_ref.shape[0]
-    for layer in range(layers):
+    low_rows = window_len * low_pos
+    start = start_ref[0]
+
+    def low_frame(frame):
+        inside = (frame >= 0) & (frame < count)
+        rank = rank_of(jnp.clip(frame, 0, count - 1), count)
+        return jnp.where(inside, tile_ref[rank], jnp.zeros((low_pos, channels), BF16))
+
+    frames = [low_frame(start + k - 1) for k in range(window_len + 2)]
+    taps = base_w_ref.shape[0]
+    shifted = [jnp.concatenate(frames[k : k + window_len], 0) for k in range(taps)]
+    total = dot(
+        jnp.concatenate(shifted, 1), base_w_ref[...].reshape(taps * channels, channels)
+    )
+    base = (shifted[1].astype(F32) + silu(total)).astype(BF16)
+    cond = dot(base, cond_w_ref[...])
+    ratio = tile_pos // low_pos
+    for k in range(ratio):
+        state_ref[pl.ds(k, low_rows, stride=ratio), :] = cond
+    state = state_ref[...] + projected_ref[...]
+    for layer in range(gains_ref.shape[0]):
         inverse = lax.rsqrt(jnp.mean(state * state, axis=-1, keepdims=True) + 1e-06)
-        normed = (state * inverse * gains_ref[layer : layer + 1, :]).reshape(
-            window_len, tile_pos, channels
+        scaled = state * inverse
+        gain = gains_ref[layer : layer + 1, :]
+        previous, same, following = (
+            gain * tconv_ref[layer, 0:1, :],
+            gain * (1.0 + tconv_ref[layer, 1:2, :]),
+            gain * tconv_ref[layer, 2:3, :],
         )
-        edge = jnp.zeros((1, tile_pos, channels), F32)
-        before = jnp.concatenate([edge, normed[:-1]], 0)
-        behind = jnp.concatenate([normed[1:], edge], 0)
-        mixed = (
-            normed
-            + tconv_ref[layer, 0:1, :] * before
-            + tconv_ref[layer, 1:2, :] * normed
-            + tconv_ref[layer, 2:3, :] * behind
-        )
-        mixed = mixed.reshape(rows, channels).astype(BF16)
-        pieces = []
-        step = rows // CHUNKS
-        for piece in range(CHUNKS):
-            part = slice(piece * step, (piece + 1) * step)
-            hidden = silu(dot(mixed[part], mlp_in_ref[layer])).astype(BF16)
-            pieces.append(state[part] + dot(hidden, mlp_out_ref[layer]))
-        state = jnp.concatenate(pieces, 0) if len(pieces) > 1 else pieces[0]
-    for copy in copies:
-        copy.wait()
-    start = starts_sm[assign_sm[lax.axis_index("frame")] // tiles]
+        block = [scaled[k * tile_pos : (k + 1) * tile_pos] for k in range(window_len)]
+        parts = []
+        for k in range(window_len):
+            mixed = same * block[k]
+            if k > 0:
+                mixed = mixed + previous * block[k - 1]
+            if k + 1 < window_len:
+                mixed = mixed + following * block[k + 1]
+            parts.append(mixed.astype(BF16))
+        half = (0.5 * dot(jnp.concatenate(parts, 0), mlp_in_ref[layer])).astype(BF16)
+        hidden = half + half * jnp.tanh(half)
+        state = state + dot(hidden, mlp_out_ref[layer])
     refined = state.astype(BF16).reshape(window_len, tile_pos, channels)
     for frame in range(window_len):
         placed_ref[rank_of(start + frame, count)] = refined[frame]
-
-
-CHUNKS = 4
 
 
 def blend_kernel(received_ref, weights_ref, video_ref):
@@ -207,17 +197,17 @@
     gathered = exchange(outgoing)
 
     moved = (base_w, cond_w, gains, tconv, mlp_in, mlp_out)
-    projected, picker, weights, zeros, *params = pl.pallas_call(
+    projected, weights, zeros, first, *params = pl.pallas_call(
         functools.partial(side_kernel, tiles),
         out_shape=(
             VMEM((rows, channels), F32),
-            VMEM((rows, count * low_pos), BF16),
             VMEM((count, tiles, channels), F32),
             VMEM((count, tile_pos, channels), BF16),
+            SMEM((1,), jnp.int32),
             *(VMEM(array.shape, array.dtype) for array in moved),
         ),
         in_specs=[spec(SMEM)] * 3 + [spec(VMEM)] * 2 + [spec(pl.ANY)] * len(moved),
-        out_specs=(spec(VMEM),) * (4 + len(moved)),
+        out_specs=(*(spec(VMEM),) * 3, spec(SMEM), *(spec(VMEM),) * len(moved)),
         scratch_shapes=[pltpu.SemaphoreType.DMA((len(moved),))],
         cost_estimate=pl.CostEstimate(
             flops=2 * rows * channels * channels, bytes_accessed=4 * rows * channels, transcendentals=0
@@ -227,16 +217,12 @@
     )(*far(assign, starts, blend, noisy, noise_w, *moved))
 
     placed = pl.pallas_call(
-        functools.partial(refine_kernel, tiles),
+        refine_kernel,
         out_shape=VMEM((count, tile_pos, channels), BF16),
-        in_specs=[spec(pl.ANY)] * 2 + [spec(VMEM)] * 10,
+        in_specs=[spec(SMEM)] + [spec(VMEM)] * 9,
         out_specs=spec(VMEM),
-        scratch_shapes=[
-            SMEM(assign.shape, jnp.int32),
-            SMEM(starts.shape, jnp.int32),
-            pltpu.SemaphoreType.DMA((2,)),
-        ],
-        input_output_aliases={11: 0},
+        scratch_shapes=[VMEM((rows, channels), F32)],
+        input_output_aliases={9: 0},
         cost_estimate=pl.CostEstimate(
             flops=4 * layers * rows * channels * hidden,
             bytes_accessed=4 * layers * channels * hidden,
@@ -245,8 +231,8 @@
         compiler_params=pltpu.CompilerParams(vmem_limit_bytes=ROOM),
         name="refine",
     )(
-        *far(assign, starts),
-        *near(gathered, projected, picker, *params, zeros),
+        first,
+        *near(gathered, projected, *params, zeros),
     )
     received = exchange(placed)
     return pl.pallas_call(

time: 30.2 us -> 28.4 us (0.940)
  Pallas kernels: 7.81 us -> 5.99 us
    pallas_call x1, Pallas kernels: 3.4 us -> 1.58 us  [on_device(): pl.pallas_call(refine_kernel, out_shape=VMEM((count, tile_pos, channels),...]
  transfers between devices with their start and end apart: 1 -> 1, of which waited for: 1 -> 1; matrix products, arithmetic and copies ran while one was open for 0% -> 0% of each run, Pallas kernels for 7% -> 8%
where the time goes in v4:
time: 28.4 us; the launch traced here: 28 us
  blocking collectives  11.8 us (42%)
  starting transfers between devices  7.89 us (28%)
  Pallas kernels  5.99 us (21%)
  waiting for transfers between devices  2.4 us (8%)
    all_to_all x1, blocking collectives, exchange(): lax.all_to_all(blocks, 'frame', split_axis=0, concat_axis=0, tiled=True,...  11.8 us
    all_to_all x1, starting transfers between devices, exchange(): lax.all_to_all(blocks, 'frame', split_axis=0, concat_axis=0, tiled=True,...  7.89 us
    all_to_all x1, waiting for transfers between devices, exchange(): lax.all_to_all(blocks, 'frame', split_axis=0, concat_axis=0, tiled=True,...  2.4 us
    pallas_call x1, Pallas kernels, on_device(): pl.pallas_call(functools.partial(side_kernel, tiles), out_shape=(VMEM((ro...  2.21 us
    pallas_call x1, Pallas kernels, on_device(): pl.pallas_call(refine_kernel, out_shape=VMEM((count, tile_pos, channels),...  1.58 us
    pallas_call x1, Pallas kernels, on_device(): pl.pallas_call(functools.partial(pick_kernel, tiles), out_shape=VMEM((cou...  1.4 us
    pallas_call x1, Pallas kernels, on_device(): pl.pallas_call(blend_kernel, out_shape=jax.ShapeDtypeStruct((1, tiles * t...  0.79 us
  transfers between devices with their start and end apart: 1, of which 1 were waited for; matrix products, arithmetic and copies ran while one was open for 0% of the time, Pallas kernels for 8%

profile of v4, /device:TPU:0, one launch (start us, length us, event | category | flops | bytes accessed | tf_op | source)
XLA Modules:
  0.0 28.0 jit_solution(2656578968000003547)
XLA Ops:
  0.0 1.4 %pick.1 = bf16[16,16,128]{2,1,0:T(8,128)(2,1)} custom-call(s32[16]{0:T(128)} %assign_ref.3, bf16[1,64,128]{2,1,0:T(8,128)(2,1)} %low_ref.1), custom_call_target="tpu_custom_call" | custom-call | tf_op jit(solution)/shard_map/pick/pallas_call | solution.py:189
  1.4 7.9 %all-to-all-start = ((bf16[16,16,128]{2,1,0:T(8,128)(2,1)}), bf16[16,16,128]{2,1,0:T(8,128)(2,1)S(1)}, u32[]{:S(2)}, u32[]{:S(2)}) async-start(bf16[16,16,128]{2,1,0:T(8,128)(2,1)} %pick.1), calls=%async_computation | async-start | bytes 131072 | tf_op jit(solution)/shard_map/all_to_all | solution.py:45
  9.3 2.2 %side.1 = (f32[512,128]{1,0:T(8,128)S(1)}, f32[16,4,128]{2,1,0:T(4,128)S(1)}, bf16[16,64,128]{2,1,0:T(8,128)(2,1)S(1)}, s32[1]{0:T(128)S(4)}, bf16[3,128,128]{2,...) custom-call(s32[16]{0:T(128)} %assign_ref.3, ...), custom_call_target="tpu_custom_call" | custom-call | flops 16777216 | bytes 262144 | tf_op jit(solution)/shard_map/side/pallas_call | solution.py:200
  11.5 2.4 %all-to-all-done.tile_ref = bf16[16,16,128]{2,1,0:T(8,128)(2,1)S(1)} async-done(((bf16[16,16,128]{2,1,0:T(8,128)(2,1)}), bf16[16,16,128]{2,1,0:T(8,128)(2,1)S(1)}, u32[]{:S(2)}, u32[]{:S(2)}) %all-to-all-start) | async-done | bytes 65568 | tf_op jit(solution)/shard_map/all_to_all | solution.py:45
  13.9 1.6 %refine.1 = bf16[16,64,128]{2,1,0:T(8,128)(2,1)S(1)} custom-call(s32[1]{0:T(128)S(4)} %get-tuple-element.15.start_ref, bf16[16,16,128]{2,1,0:T(8,128)(2,1)S(1)} %all-to-all-done.tile_ref, f32[512,128]{1,0:T(8,128)S(1)} %get-tuple-element.16.projected_ref, bf16[3,128,128]{2,1,0:T(8,128)(2,1)S(1)} %get-tuple-element.17.base_w_ref, ...), custom_call_target="tpu_custom_call", output_to_operand_aliasing={{}: (9, {})} | custom-call | flops 402653184 | bytes 786432 | tf_op jit(solution)/shard_map/refine/pallas_call | solution.py:219
  15.5 11.8 %all_to_all.10.received_ref = bf16[16,64,128]{2,1,0:T(8,128)(2,1)S(1)} all-to-all(bf16[16,64,128]{2,1,0:T(8,128)(2,1)S(1)} %refine.1), channel_id=1, replica_groups={{8,9,10,11,12,13,14,15,0,1,2,3,4,5,6,7},{24,25,26,27,28,29,30,31,16,17,..., dimensions={0} | all-to-all | bytes 524288 | tf_op jit(solution)/shard_map/all_to_all | solution.py:45
  27.3 0.8 %blend.1 = bf16[1,256,128]{2,1,0:T(8,128)(2,1)} custom-call(bf16[16,64,128]{2,1,0:T(8,128)(2,1)S(1)} %all_to_all.10.received_ref, f32[16,4,128]{2,1,0:T(4,128)S(1)} %get-tuple-element.24.weights_ref), custom_call_target="tpu_custom_call" | custom-call | tf_op jit(solution)/shard_map/blend/pallas_call | solution.py:238
Async XLA Ops:
  1.4 12.5 %all-to-all-start = ((bf16[16,16,128]{2,1,0:T(8,128)(2,1)}), bf16[16,16,128]{2,1,0:T(8,128)(2,1)S(1)}, u32[]{:S(2)}, u32[]{:S(2)}) async-start(bf16[16,16,128]{2,1,0:T(8,128)(2,1)} %pick.1), calls=%async_computation | async-start | bytes 131072 | tf_op jit(solution)/shard_map/all_to_all | solution.py:45

commit v5 on v4

--- a/solution.py
+++ b/solution.py
@@ -35,13 +35,21 @@
     return tuple(pltpu.with_memory_space_constraint(array, pltpu.HBM) for array in arrays)
 
 
-def rank_of(frame, count):
-    return lax.rem(frame + count // 2, jnp.int32(count))
-
-
-def exchange(blocks):
+FIRST = (2, 0, 1, 3)
+SECOND = (2, 0, 1, 3)
+
+
+def rank_of(frame, count, quarters):
+    quarter = count // 4
+    block, rest = frame // quarter, lax.rem(frame, quarter)
+    place = sum(jnp.where(block == q, spot, 0) for spot, q in enumerate(quarters))
+    return place * quarter + quarter - 1 - rest
+
+
+def exchange(blocks, quarters):
     count = blocks.shape[0]
-    order = [(rank + count // 2) % count for rank in range(count)]
+    quarter = count // 4
+    order = [q * quarter + k for q in quarters for k in reversed(range(quarter))]
     return lax.all_to_all(
         blocks, "frame", split_axis=0, concat_axis=0, tiled=True, axis_index_groups=[order]
     )
@@ -53,7 +61,7 @@
     def body(slot, carry):
         tile = lax.rem(assign_ref[slot], tiles)
         first = pl.multiple_of(tile * low_pos, low_pos)
-        out_ref[rank_of(slot, count)] = low_ref[0, pl.ds(first, low_pos), :]
+        out_ref[rank_of(slot, count, FIRST)] = low_ref[0, pl.ds(first, low_pos), :]
         return carry
 
     lax.fori_loop(0, count, body, 0, unroll=min(count, 16))
@@ -64,7 +72,7 @@
 ):
     moved = (len(refs) - 5) // 2
     sources, targets, sems = refs[:moved], refs[moved + 4 : -1], refs[-1]
-    projected_ref, weights_ref, placed_ref, start_ref = refs[moved : moved + 4]
+    projected_ref, weights_ref, placed_ref, spots_ref = refs[moved : moved + 4]
     copies = [
         pltpu.make_async_copy(source, target, sems.at[k])
         for k, (source, target) in enumerate(zip(sources, targets))
@@ -78,7 +86,13 @@
     rows = projected_ref.shape[0]
     own = lax.axis_index("frame")
     projected_ref[...] = dot(noisy_ref[0].reshape(rows, channels), noise_w_ref[...])
-    start_ref[0] = starts_ref[assign_ref[own] // tiles]
+    start = starts_ref[assign_ref[own] // tiles]
+    for k in range(window_len + 2):
+        frame = start + k - 1
+        inside = (frame >= 0) & (frame < count)
+        near_frame = jnp.clip(frame, 0, count - 1)
+        spots_ref[k] = jnp.where(inside, rank_of(near_frame, count, FIRST), -1)
+        spots_ref[window_len + 2 + k] = rank_of(near_frame, count, SECOND)
     placed_ref[...] = jnp.zeros_like(placed_ref)
 
     def factor_of(window):
@@ -97,7 +111,8 @@
         item = assign_ref[slot]
         factor = factor_of(item // tiles)
         factor_row = jnp.full((1, channels), factor, jnp.int32).astype(F32)
-        weights_ref[rank_of(slot, count), pl.ds(lax.rem(item, tiles), 1), :] = factor_row / denom_row
+        spot = rank_of(slot, count, SECOND)
+        weights_ref[spot, pl.ds(lax.rem(item, tiles), 1), :] = factor_row / denom_row
         return carry
 
     lax.fori_loop(0, count, body, 0)
@@ -106,22 +121,23 @@
 
 
 def refine_kernel(
-    start_ref, tile_ref, projected_ref, base_w_ref, cond_w_ref, gains_ref, tconv_ref, mlp_in_ref,
+    spots_ref, tile_ref, projected_ref, base_w_ref, cond_w_ref, gains_ref, tconv_ref, mlp_in_ref,
     mlp_out_ref, zeros_ref, placed_ref, state_ref,
 ):
-    count, low_pos, channels = tile_ref.shape
+    _, low_pos, channels = tile_ref.shape
     rows = projected_ref.shape[0]
     tile_pos = placed_ref.shape[1]
     window_len = rows // tile_pos
     low_rows = window_len * low_pos
-    start = start_ref[0]
-
-    def low_frame(frame):
-        inside = (frame >= 0) & (frame < count)
-        rank = rank_of(jnp.clip(frame, 0, count - 1), count)
-        return jnp.where(inside, tile_ref[rank], jnp.zeros((low_pos, channels), BF16))
-
-    frames = [low_frame(start + k - 1) for k in range(window_len + 2)]
+
+    def low_frame(k):
+        spot = spots_ref[k]
+        frame = tile_ref[jnp.maximum(spot, 0)]
+        if 0 < k <= window_len:
+            return frame
+        return jnp.where(spot >= 0, frame, jnp.zeros_like(frame))
+
+    frames = [low_frame(k) for k in range(window_len + 2)]
     taps = base_w_ref.shape[0]
     shifted = [jnp.concatenate(frames[k : k + window_len], 0) for k in range(taps)]
     total = dot(
@@ -156,7 +172,7 @@
         state = state + dot(hidden, mlp_out_ref[layer])
     refined = state.astype(BF16).reshape(window_len, tile_pos, channels)
     for frame in range(window_len):
-        placed_ref[rank_of(start + frame, count)] = refined[frame]
+        placed_ref[spots_ref[window_len + 3 + frame]] = refined[frame]
 
 
 def blend_kernel(received_ref, weights_ref, video_ref):
@@ -194,16 +210,16 @@
         compiler_params=pltpu.CompilerParams(vmem_limit_bytes=ROOM),
         name="pick",
     )(*far(assign, lowres))
-    gathered = exchange(outgoing)
+    gathered = exchange(outgoing, FIRST)
 
     moved = (base_w, cond_w, gains, tconv, mlp_in, mlp_out)
-    projected, weights, zeros, first, *params = pl.pallas_call(
+    projected, weights, zeros, spots, *params = pl.pallas_call(
         functools.partial(side_kernel, tiles),
         out_shape=(
             VMEM((rows, channels), F32),
             VMEM((count, tiles, channels), F32),
             VMEM((count, tile_pos, channels), BF16),
-            SMEM((1,), jnp.int32),
+            SMEM((2 * (window_len + 2),), jnp.int32),
             *(VMEM(array.shape, array.dtype) for array in moved),
         ),
         in_specs=[spec(SMEM)] * 3 + [spec(VMEM)] * 2 + [spec(pl.ANY)] * len(moved),
@@ -231,10 +247,10 @@
         compiler_params=pltpu.CompilerParams(vmem_limit_bytes=ROOM),
         name="refine",
     )(
-        first,
+        spots,
         *near(gathered, projected, *params, zeros),
     )
-    received = exchange(placed)
+    received = exchange(placed, SECOND)
     return pl.pallas_call(
         blend_kernel,
         out_shape=jax.ShapeDtypeStruct((1, tiles * tile_pos, channels), BF16),

time: 28.4 us -> 26.1 us (0.919)
  the two profiles are of different devices: /device:TPU:0 before, /device:TPU:1 now
where the time goes in v5:
time: 26.1 us; the launch traced here: 25.8 us
  blocking collectives  11.1 us (43%)
  starting transfers between devices  7.41 us (28%)
  Pallas kernels  6.02 us (23%)
  waiting for transfers between devices  1.21 us (5%)
    all_to_all x1, blocking collectives, exchange(): lax.all_to_all(blocks, 'frame', split_axis=0, concat_axis=0, tiled=True,...  11.1 us
    all_to_all x1, starting transfers between devices, exchange(): lax.all_to_all(blocks, 'frame', split_axis=0, concat_axis=0, tiled=True,...  7.41 us
    pallas_call x1, Pallas kernels, on_device(): pl.pallas_call(functools.partial(side_kernel, tiles), out_shape=(VMEM((ro...  2.24 us
    pallas_call x1, Pallas kernels, on_device(): pl.pallas_call(refine_kernel, out_shape=VMEM((count, tile_pos, channels),...  1.59 us
    pallas_call x1, Pallas kernels, on_device(): pl.pallas_call(functools.partial(pick_kernel, tiles), out_shape=VMEM((cou...  1.4 us
    all_to_all x1, waiting for transfers between devices, exchange(): lax.all_to_all(blocks, 'frame', split_axis=0, concat_axis=0, tiled=True,...  1.21 us
    pallas_call x1, Pallas kernels, on_device(): pl.pallas_call(blend_kernel, out_shape=jax.ShapeDtypeStruct((1, tiles * t...  0.79 us
  transfers between devices with their start and end apart: 1, of which 1 were waited for; matrix products, arithmetic and copies ran while one was open for 0% of the time, Pallas kernels for 9%

profile of v5, /device:TPU:1, one launch (start us, length us, event | category | flops | bytes accessed | tf_op | source)
XLA Modules:
  0.0 25.8 jit_solution(6949601302123008929)
XLA Ops:
  0.0 1.4 %pick.1 = bf16[16,16,128]{2,1,0:T(8,128)(2,1)} custom-call(s32[16]{0:T(128)} %assign_ref.3, bf16[1,64,128]{2,1,0:T(8,128)(2,1)} %low_ref.1), custom_call_target="tpu_custom_call" | custom-call | tf_op jit(solution)/shard_map/pick/pallas_call | solution.py:205
  1.4 7.4 %all-to-all-start = ((bf16[16,16,128]{2,1,0:T(8,128)(2,1)}), bf16[16,16,128]{2,1,0:T(8,128)(2,1)S(1)}, u32[]{:S(2)}, u32[]{:S(2)}) async-start(bf16[16,16,128]{2,1,0:T(8,128)(2,1)} %pick.1), calls=%async_computation | async-start | bytes 131072 | tf_op jit(solution)/shard_map/all_to_all | solution.py:53
  8.8 2.2 %side.1 = (f32[512,128]{1,0:T(8,128)S(1)}, f32[16,4,128]{2,1,0:T(4,128)S(1)}, bf16[16,64,128]{2,1,0:T(8,128)(2,1)S(1)}, s32[20]{0:T(128)S(4)}, bf16[3,128,128]{2...) custom-call(s32[16]{0:T(128)} %assign_ref.3, ...), custom_call_target="tpu_custom_call" | custom-call | flops 16777216 | bytes 262144 | tf_op jit(solution)/shard_map/side/pallas_call | solution.py:216
  11.1 1.2 %all-to-all-done.tile_ref = bf16[16,16,128]{2,1,0:T(8,128)(2,1)S(1)} async-done(((bf16[16,16,128]{2,1,0:T(8,128)(2,1)}), bf16[16,16,128]{2,1,0:T(8,128)(2,1)S(1)}, u32[]{:S(2)}, u32[]{:S(2)}) %all-to-all-start) | async-done | bytes 65568 | tf_op jit(solution)/shard_map/all_to_all | solution.py:53
  12.3 1.6 %refine.1 = bf16[16,64,128]{2,1,0:T(8,128)(2,1)S(1)} custom-call(s32[20]{0:T(128)S(4)} %get-tuple-element.15.spots_ref, bf16[16,16,128]{2,1,0:T(8,128)(2,1)S(1)} %all-to-all-done.tile_ref, f32[512,128]{1,0:T(8,128)S(1)} %get-tuple-element.16.projected_ref, bf16[3,128,128]{2,1,0:T(8,128)(2,1)S(1)} %get-tuple-element.17.base_w_ref, ...), custom_call_target="tpu_custom_call", output_to_operand_aliasing={{}: (9, {})} | custom-call | flops 402653184 | bytes 786432 | tf_op jit(solution)/shard_map/refine/pallas_call | solution.py:235
  13.9 11.1 %all_to_all.10.received_ref = bf16[16,64,128]{2,1,0:T(8,128)(2,1)S(1)} all-to-all(bf16[16,64,128]{2,1,0:T(8,128)(2,1)S(1)} %refine.1), channel_id=1, replica_groups={{11,10,9,8,3,2,1,0,7,6,5,4,15,14,13,12},{27,26,25,24,19,18,17,16,23,22,..., dimensions={0} | all-to-all | bytes 524288 | tf_op jit(solution)/shard_map/all_to_all | solution.py:53
  25.0 0.8 %blend.1 = bf16[1,256,128]{2,1,0:T(8,128)(2,1)} custom-call(bf16[16,64,128]{2,1,0:T(8,128)(2,1)S(1)} %all_to_all.10.received_ref, f32[16,4,128]{2,1,0:T(4,128)S(1)} %get-tuple-element.24.weights_ref), custom_call_target="tpu_custom_call" | custom-call | tf_op jit(solution)/shard_map/blend/pallas_call | solution.py:254
Async XLA Ops:
  1.4 10.9 %all-to-all-start = ((bf16[16,16,128]{2,1,0:T(8,128)(2,1)}), bf16[16,16,128]{2,1,0:T(8,128)(2,1)S(1)}, u32[]{:S(2)}, u32[]{:S(2)}) async-start(bf16[16,16,128]{2,1,0:T(8,128)(2,1)} %pick.1), calls=%async_computation | async-start | bytes 131072 | tf_op jit(solution)/shard_map/all_to_all | solution.py:53

commit v6 on v5

--- a/solution.py
+++ b/solution.py
@@ -35,21 +35,24 @@
     return tuple(pltpu.with_memory_space_constraint(array, pltpu.HBM) for array in arrays)
 
 
-FIRST = (2, 0, 1, 3)
-SECOND = (2, 0, 1, 3)
-
-
-def rank_of(frame, count, quarters):
-    quarter = count // 4
-    block, rest = frame // quarter, lax.rem(frame, quarter)
-    place = sum(jnp.where(block == q, spot, 0) for spot, q in enumerate(quarters))
-    return place * quarter + quarter - 1 - rest
-
-
-def exchange(blocks, quarters):
-    count = blocks.shape[0]
-    quarter = count // 4
-    order = [q * quarter + k for q in quarters for k in reversed(range(quarter))]
+FIRST = (11, 10, 9, 8, 3, 2, 1, 0, 7, 6, 5, 4, 15, 14, 13, 12)
+SECOND = (11, 10, 9, 8, 13, 6, 1, 0, 7, 12, 5, 4, 15, 3, 2, 14)
+
+
+def order_of(count, cells):
+    width = count // len(cells)
+    if width * len(cells) != count:
+        return list(range(count))
+    return [cell * width + k for cell in cells for k in range(width)]
+
+
+def ranks_of(count, cells):
+    order = order_of(count, cells)
+    return [order.index(frame) for frame in range(count)]
+
+
+def exchange(blocks, cells):
+    order = order_of(blocks.shape[0], cells)
     return lax.all_to_all(
         blocks, "frame", split_axis=0, concat_axis=0, tiled=True, axis_index_groups=[order]
     )
@@ -57,21 +60,17 @@
 
 def pick_kernel(tiles, assign_ref, low_ref, out_ref):
     count, low_pos, _ = out_ref.shape
-
-    def body(slot, carry):
+    for slot, rank in enumerate(ranks_of(count, FIRST)):
         tile = lax.rem(assign_ref[slot], tiles)
         first = pl.multiple_of(tile * low_pos, low_pos)
-        out_ref[rank_of(slot, count, FIRST)] = low_ref[0, pl.ds(first, low_pos), :]
-        return carry
-
-    lax.fori_loop(0, count, body, 0, unroll=min(count, 16))
+        out_ref[rank] = low_ref[0, pl.ds(first, low_pos), :]
 
 
 def side_kernel(
     tiles, assign_ref, starts_ref, blend_ref, noisy_ref, noise_w_ref, *refs
 ):
-    moved = (len(refs) - 5) // 2
-    sources, targets, sems = refs[:moved], refs[moved + 4 : -1], refs[-1]
+    moved = (len(refs) - 6) // 2
+    sources, targets, ranks_ref, sems = refs[:moved], refs[moved + 4 : -2], refs[-2], refs[-1]
     projected_ref, weights_ref, placed_ref, spots_ref = refs[moved : moved + 4]
     copies = [
         pltpu.make_async_copy(source, target, sems.at[k])
@@ -86,13 +85,16 @@
     rows = projected_ref.shape[0]
     own = lax.axis_index("frame")
     projected_ref[...] = dot(noisy_ref[0].reshape(rows, channels), noise_w_ref[...])
+    for side, cells in enumerate((FIRST, SECOND)):
+        for frame, rank in enumerate(ranks_of(count, cells)):
+            ranks_ref[side * count + frame] = rank
     start = starts_ref[assign_ref[own] // tiles]
     for k in range(window_len + 2):
         frame = start + k - 1
         inside = (frame >= 0) & (frame < count)
         near_frame = jnp.clip(frame, 0, count - 1)
-        spots_ref[k] = jnp.where(inside, rank_of(near_frame, count, FIRST), -1)
-        spots_ref[window_len + 2 + k] = rank_of(near_frame, count, SECOND)
+        spots_ref[k] = jnp.where(inside, ranks_ref[near_frame], -1)
+        spots_ref[window_len + 2 + k] = ranks_ref[count + near_frame]
     placed_ref[...] = jnp.zeros_like(placed_ref)
 
     def factor_of(window):
@@ -111,7 +113,7 @@
         item = assign_ref[slot]
         factor = factor_of(item // tiles)
         factor_row = jnp.full((1, channels), factor, jnp.int32).astype(F32)
-        spot = rank_of(slot, count, SECOND)
+        spot = ranks_ref[count + slot]
         weights_ref[spot, pl.ds(lax.rem(item, tiles), 1), :] = factor_row / denom_row
         return carry
 
@@ -152,7 +154,7 @@
     for layer in range(gains_ref.shape[0]):
         inverse = lax.rsqrt(jnp.mean(state * state, axis=-1, keepdims=True) + 1e-06)
         scaled = state * inverse
-        gain = gains_ref[layer : layer + 1, :]
+        gain = 0.5 * gains_ref[layer : layer + 1, :]
         previous, same, following = (
             gain * tconv_ref[layer, 0:1, :],
             gain * (1.0 + tconv_ref[layer, 1:2, :]),
@@ -167,8 +169,8 @@
             if k + 1 < window_len:
                 mixed = mixed + following * block[k + 1]
             parts.append(mixed.astype(BF16))
-        half = (0.5 * dot(jnp.concatenate(parts, 0), mlp_in_ref[layer])).astype(BF16)
-        hidden = half + half * jnp.tanh(half)
+        half = dot(jnp.concatenate(parts, 0), mlp_in_ref[layer])
+        hidden = (half + half * jnp.tanh(half)).astype(BF16)
         state = state + dot(hidden, mlp_out_ref[layer])
     refined = state.astype(BF16).reshape(window_len, tile_pos, channels)
     for frame in range(window_len):
@@ -224,7 +226,10 @@
         ),
         in_specs=[spec(SMEM)] * 3 + [spec(VMEM)] * 2 + [spec(pl.ANY)] * len(moved),
         out_specs=(*(spec(VMEM),) * 3, spec(SMEM), *(spec(VMEM),) * len(moved)),
-        scratch_shapes=[pltpu.SemaphoreType.DMA((len(moved),))],
+        scratch_shapes=[
+            SMEM((2 * count,), jnp.int32),
+            pltpu.SemaphoreType.DMA((len(moved),)),
+        ],
         cost_estimate=pl.CostEstimate(
             flops=2 * rows * channels * channels, bytes_accessed=4 * rows * channels, transcendentals=0
         ),

time: 26.1 us -> 25.8 us (0.989)
  blocking collectives: 11.1 us -> 10.8 us
    all_to_all x1, blocking collectives: 11.1 us -> 10.8 us  [exchange(): lax.all_to_all(blocks, 'frame', split_axis=0, concat_axis=0, tiled=True,...]
where the time goes in v6:
time: 25.8 us; the launch traced here: 25.5 us
  blocking collectives  10.8 us (42%)
  starting transfers between devices  7.41 us (29%)
  Pallas kernels  6.02 us (23%)
  waiting for transfers between devices  1.21 us (5%)
    all_to_all x1, blocking collectives, exchange(): lax.all_to_all(blocks, 'frame', split_axis=0, concat_axis=0, tiled=True,...  10.8 us
    all_to_all x1, starting transfers between devices, exchange(): lax.all_to_all(blocks, 'frame', split_axis=0, concat_axis=0, tiled=True,...  7.41 us
    pallas_call x1, Pallas kernels, on_device(): pl.pallas_call(functools.partial(side_kernel, tiles), out_shape=(VMEM((ro...  2.24 us
    pallas_call x1, Pallas kernels, on_device(): pl.pallas_call(refine_kernel, out_shape=VMEM((count, tile_pos, channels),...  1.59 us
    pallas_call x1, Pallas kernels, on_device(): pl.pallas_call(functools.partial(pick_kernel, tiles), out_shape=VMEM((cou...  1.4 us
    all_to_all x1, waiting for transfers between devices, exchange(): lax.all_to_all(blocks, 'frame', split_axis=0, concat_axis=0, tiled=True,...  1.21 us
    pallas_call x1, Pallas kernels, on_device(): pl.pallas_call(blend_kernel, out_shape=jax.ShapeDtypeStruct((1, tiles * t...  0.79 us
  transfers between devices with their start and end apart: 1, of which 1 were waited for; matrix products, arithmetic and copies ran while one was open for 0% of the time, Pallas kernels for 9%

profile of v6, /device:TPU:1, one launch (start us, length us, event | category | flops | bytes accessed | tf_op | source)
XLA Modules:
  0.0 25.5 jit_solution(3639265316322034350)
XLA Ops:
  0.0 1.4 %pick.1 = bf16[16,16,128]{2,1,0:T(8,128)(2,1)} custom-call(s32[16]{0:T(128)} %assign_ref.3, bf16[1,64,128]{2,1,0:T(8,128)(2,1)} %low_ref.1), custom_call_target="tpu_custom_call" | custom-call | tf_op jit(solution)/shard_map/pick/pallas_call | solution.py:207
  1.4 7.4 %all-to-all-start = ((bf16[16,16,128]{2,1,0:T(8,128)(2,1)}), bf16[16,16,128]{2,1,0:T(8,128)(2,1)S(1)}, u32[]{:S(2)}, u32[]{:S(2)}) async-start(bf16[16,16,128]{2,1,0:T(8,128)(2,1)} %pick.1), calls=%async_computation | async-start | bytes 131072 | tf_op jit(solution)/shard_map/all_to_all | solution.py:56
  8.8 2.2 %side.1 = (f32[512,128]{1,0:T(8,128)S(1)}, f32[16,4,128]{2,1,0:T(4,128)S(1)}, bf16[16,64,128]{2,1,0:T(8,128)(2,1)S(1)}, s32[20]{0:T(128)S(4)}, bf16[3,128,128]{2...) custom-call(s32[16]{0:T(128)} %assign_ref.3, ...), custom_call_target="tpu_custom_call" | custom-call | flops 16777216 | bytes 262144 | tf_op jit(solution)/shard_map/side/pallas_call | solution.py:218
  11.1 1.2 %all-to-all-done.tile_ref = bf16[16,16,128]{2,1,0:T(8,128)(2,1)S(1)} async-done(((bf16[16,16,128]{2,1,0:T(8,128)(2,1)}), bf16[16,16,128]{2,1,0:T(8,128)(2,1)S(1)}, u32[]{:S(2)}, u32[]{:S(2)}) %all-to-all-start) | async-done | bytes 65568 | tf_op jit(solution)/shard_map/all_to_all | solution.py:56
  12.3 1.6 %refine.1 = bf16[16,64,128]{2,1,0:T(8,128)(2,1)S(1)} custom-call(s32[20]{0:T(128)S(4)} %get-tuple-element.15.spots_ref, bf16[16,16,128]{2,1,0:T(8,128)(2,1)S(1)} %all-to-all-done.tile_ref, f32[512,128]{1,0:T(8,128)S(1)} %get-tuple-element.16.projected_ref, bf16[3,128,128]{2,1,0:T(8,128)(2,1)S(1)} %get-tuple-element.17.base_w_ref, ...), custom_call_target="tpu_custom_call", output_to_operand_aliasing={{}: (9, {})} | custom-call | flops 402653184 | bytes 786432 | tf_op jit(solution)/shard_map/refine/pallas_call | solution.py:240
  13.9 10.8 %all_to_all.10.received_ref = bf16[16,64,128]{2,1,0:T(8,128)(2,1)S(1)} all-to-all(bf16[16,64,128]{2,1,0:T(8,128)(2,1)S(1)} %refine.1), channel_id=1, replica_groups={{11,10,9,8,13,6,1,0,7,12,5,4,15,3,2,14},{27,26,25,24,29,22,17,16,23,28,..., dimensions={0} | all-to-all | bytes 524288 | tf_op jit(solution)/shard_map/all_to_all | solution.py:56
  24.7 0.8 %blend.1 = bf16[1,256,128]{2,1,0:T(8,128)(2,1)} custom-call(bf16[16,64,128]{2,1,0:T(8,128)(2,1)S(1)} %all_to_all.10.received_ref, f32[16,4,128]{2,1,0:T(4,128)S(1)} %get-tuple-element.24.weights_ref), custom_call_target="tpu_custom_call" | custom-call | tf_op jit(solution)/shard_map/blend/pallas_call | solution.py:259
Async XLA Ops:
  1.4 10.9 %all-to-all-start = ((bf16[16,16,128]{2,1,0:T(8,128)(2,1)}), bf16[16,16,128]{2,1,0:T(8,128)(2,1)S(1)}, u32[]{:S(2)}, u32[]{:S(2)}) async-start(bf16[16,16,128]{2,1,0:T(8,128)(2,1)} %pick.1), calls=%async_computation | async-start | bytes 131072 | tf_op jit(solution)/shard_map/all_to_all | solution.py:56

commit v7 on v6

--- a/solution.py
+++ b/solution.py
@@ -36,7 +36,7 @@
 
 
 FIRST = (11, 10, 9, 8, 3, 2, 1, 0, 7, 6, 5, 4, 15, 14, 13, 12)
-SECOND = (11, 10, 9, 8, 13, 6, 1, 0, 7, 12, 5, 4, 15, 3, 2, 14)
+SECOND = (11, 10, 4, 8, 13, 6, 15, 0, 7, 1, 5, 12, 9, 3, 2, 14)
 
 
 def order_of(count, cells):
@@ -150,7 +150,7 @@
     ratio = tile_pos // low_pos
     for k in range(ratio):
         state_ref[pl.ds(k, low_rows, stride=ratio), :] = cond
-    state = state_ref[...] + projected_ref[...]
+    state = state_ref[:rows] + projected_ref[...]
     for layer in range(gains_ref.shape[0]):
         inverse = lax.rsqrt(jnp.mean(state * state, axis=-1, keepdims=True) + 1e-06)
         scaled = state * inverse
@@ -242,7 +242,7 @@
         out_shape=VMEM((count, tile_pos, channels), BF16),
         in_specs=[spec(SMEM)] + [spec(VMEM)] * 9,
         out_specs=spec(VMEM),
-        scratch_shapes=[VMEM((rows, channels), F32)],
+        scratch_shapes=[VMEM((rows + 8, channels), F32)],
         input_output_aliases={9: 0},
         cost_estimate=pl.CostEstimate(
             flops=4 * layers * rows * channels * hidden,

time: 25.8 us -> 25.6 us (level)
  the two profiles are of different devices: /device:TPU:1 before, /device:TPU:0 now
where the time goes in v7:
time: 25.6 us; the launch traced here: 25.2 us
  blocking collectives  10.2 us (40%)
  starting transfers between devices  7.79 us (30%)
  Pallas kernels  6.01 us (23%)
  waiting for transfers between devices  1.2 us (5%)
    all_to_all x1, blocking collectives, exchange(): lax.all_to_all(blocks, 'frame', split_axis=0, concat_axis=0, tiled=True,...  10.2 us
    all_to_all x1, starting transfers between devices, exchange(): lax.all_to_all(blocks, 'frame', split_axis=0, concat_axis=0, tiled=True,...  7.79 us
    pallas_call x1, Pallas kernels, on_device(): pl.pallas_call(functools.partial(side_kernel, tiles), out_shape=(VMEM((ro...  2.24 us
    pallas_call x1, Pallas kernels, on_device(): pl.pallas_call(refine_kernel, out_shape=VMEM((count, tile_pos, channels),...  1.58 us
    pallas_call x1, Pallas kernels, on_device(): pl.pallas_call(functools.partial(pick_kernel, tiles), out_shape=VMEM((cou...  1.4 us
    all_to_all x1, waiting for transfers between devices, exchange(): lax.all_to_all(blocks, 'frame', split_axis=0, concat_axis=0, tiled=True,...  1.2 us
    pallas_call x1, Pallas kernels, on_device(): pl.pallas_call(blend_kernel, out_shape=jax.ShapeDtypeStruct((1, tiles * t...  0.79 us
  transfers between devices with their start and end apart: 1, of which 1 were waited for; matrix products, arithmetic and copies ran while one was open for 0% of the time, Pallas kernels for 9%

profile of v7, /device:TPU:0, one launch (start us, length us, event | category | flops | bytes accessed | tf_op | source)
XLA Modules:
  0.0 25.2 jit_solution(6037583894742576297)
XLA Ops:
  0.0 1.4 %pick.1 = bf16[16,16,128]{2,1,0:T(8,128)(2,1)} custom-call(s32[16]{0:T(128)} %assign_ref.3, bf16[1,64,128]{2,1,0:T(8,128)(2,1)} %low_ref.1), custom_call_target="tpu_custom_call" | custom-call | tf_op jit(solution)/shard_map/pick/pallas_call | solution.py:207
  1.4 7.8 %all-to-all-start = ((bf16[16,16,128]{2,1,0:T(8,128)(2,1)}), bf16[16,16,128]{2,1,0:T(8,128)(2,1)S(1)}, u32[]{:S(2)}, u32[]{:S(2)}) async-start(bf16[16,16,128]{2,1,0:T(8,128)(2,1)} %pick.1), calls=%async_computation | async-start | bytes 131072 | tf_op jit(solution)/shard_map/all_to_all | solution.py:56
  9.2 2.2 %side.1 = (f32[512,128]{1,0:T(8,128)S(1)}, f32[16,4,128]{2,1,0:T(4,128)S(1)}, bf16[16,64,128]{2,1,0:T(8,128)(2,1)S(1)}, s32[20]{0:T(128)S(4)}, bf16[3,128,128]{2...) custom-call(s32[16]{0:T(128)} %assign_ref.3, ...), custom_call_target="tpu_custom_call" | custom-call | flops 16777216 | bytes 262144 | tf_op jit(solution)/shard_map/side/pallas_call | solution.py:218
  11.4 1.2 %all-to-all-done.tile_ref = bf16[16,16,128]{2,1,0:T(8,128)(2,1)S(1)} async-done(((bf16[16,16,128]{2,1,0:T(8,128)(2,1)}), bf16[16,16,128]{2,1,0:T(8,128)(2,1)S(1)}, u32[]{:S(2)}, u32[]{:S(2)}) %all-to-all-start) | async-done | bytes 65568 | tf_op jit(solution)/shard_map/all_to_all | solution.py:56
  12.7 1.6 %refine.1 = bf16[16,64,128]{2,1,0:T(8,128)(2,1)S(1)} custom-call(s32[20]{0:T(128)S(4)} %get-tuple-element.15.spots_ref, bf16[16,16,128]{2,1,0:T(8,128)(2,1)S(1)} %all-to-all-done.tile_ref, f32[512,128]{1,0:T(8,128)S(1)} %get-tuple-element.16.projected_ref, bf16[3,128,128]{2,1,0:T(8,128)(2,1)S(1)} %get-tuple-element.17.base_w_ref, ...), custom_call_target="tpu_custom_call", output_to_operand_aliasing={{}: (9, {})} | custom-call | flops 402653184 | bytes 786432 | tf_op jit(solution)/shard_map/refine/pallas_call | solution.py:240
  14.2 10.2 %all_to_all.10.received_ref = bf16[16,64,128]{2,1,0:T(8,128)(2,1)S(1)} all-to-all(bf16[16,64,128]{2,1,0:T(8,128)(2,1)S(1)} %refine.1), channel_id=1, replica_groups={{11,10,4,8,13,6,15,0,7,1,5,12,9,3,2,14},{27,26,20,24,29,22,31,16,23,17,..., dimensions={0} | all-to-all | bytes 524288 | tf_op jit(solution)/shard_map/all_to_all | solution.py:56
  24.5 0.8 %blend.1 = bf16[1,256,128]{2,1,0:T(8,128)(2,1)} custom-call(bf16[16,64,128]{2,1,0:T(8,128)(2,1)S(1)} %all_to_all.10.received_ref, f32[16,4,128]{2,1,0:T(4,128)S(1)} %get-tuple-element.24.weights_ref), custom_call_target="tpu_custom_call" | custom-call | tf_op jit(solution)/shard_map/blend/pallas_call | solution.py:259
Async XLA Ops:
  1.4 11.2 %all-to-all-start = ((bf16[16,16,128]{2,1,0:T(8,128)(2,1)}), bf16[16,16,128]{2,1,0:T(8,128)(2,1)S(1)}, u32[]{:S(2)}, u32[]{:S(2)}) async-start(bf16[16,16,128]{2,1,0:T(8,128)(2,1)} %pick.1), calls=%async_computation | async-start | bytes 131072 | tf_op jit(solution)/shard_map/all_to_all | solution.py:56

commit v8 on v7

--- a/solution.py
+++ b/solution.py
@@ -69,9 +69,9 @@
 def side_kernel(
     tiles, assign_ref, starts_ref, blend_ref, noisy_ref, noise_w_ref, *refs
 ):
-    moved = (len(refs) - 6) // 2
-    sources, targets, ranks_ref, sems = refs[:moved], refs[moved + 4 : -2], refs[-2], refs[-1]
-    projected_ref, weights_ref, placed_ref, spots_ref = refs[moved : moved + 4]
+    moved = (len(refs) - 7) // 2
+    sources, targets, ranks_ref, sems = refs[:moved], refs[moved + 5 : -2], refs[-2], refs[-1]
+    projected_ref, weights_ref, placed_ref, spots_ref, owners_ref = refs[moved : moved + 5]
     copies = [
         pltpu.make_async_copy(source, target, sems.at[k])
         for k, (source, target) in enumerate(zip(sources, targets))
@@ -107,17 +107,11 @@
         0, windows, lambda w, total: total + factor_of(w), jnp.int32(0), unroll=min(windows, 4)
     )
     denom_row = jnp.full((1, channels), denom, jnp.int32).astype(F32)
-    weights_ref[...] = jnp.zeros_like(weights_ref)
-
-    def body(slot, carry):
-        item = assign_ref[slot]
-        factor = factor_of(item // tiles)
-        factor_row = jnp.full((1, channels), factor, jnp.int32).astype(F32)
-        spot = ranks_ref[count + slot]
-        weights_ref[spot, pl.ds(lax.rem(item, tiles), 1), :] = factor_row / denom_row
-        return carry
-
-    lax.fori_loop(0, count, body, 0)
+    for window in range(windows):
+        factor_row = jnp.full((1, channels), factor_of(window), jnp.int32).astype(F32)
+        weights_ref[window : window + 1, :] = factor_row / denom_row
+    for slot in range(count):
+        owners_ref[assign_ref[slot]] = ranks_ref[count + slot]
     for copy in copies:
         copy.wait()
 
@@ -177,19 +171,17 @@
         placed_ref[spots_ref[window_len + 3 + frame]] = refined[frame]
 
 
-def blend_kernel(received_ref, weights_ref, video_ref):
-    count, tile_pos, channels = received_ref.shape
-    tiles = weights_ref.shape[1]
-
-    def body(slot, totals):
-        rows = received_ref[slot].astype(F32)
-        weights = weights_ref[slot]
-        return tuple(totals[t] + weights[t : t + 1, :] * rows for t in range(tiles))
-
-    zero = jnp.zeros((tile_pos, channels), F32)
-    totals = lax.fori_loop(0, count, body, (zero,) * tiles, unroll=min(count, 16))
+def blend_kernel(owners_ref, received_ref, weights_ref, video_ref):
+    tile_pos = received_ref.shape[1]
+    windows = weights_ref.shape[0]
+    tiles = received_ref.shape[0] // windows
     for t in range(tiles):
-        video_ref[0, t * tile_pos : (t + 1) * tile_pos, :] = totals[t].astype(BF16)
+        total = None
+        for window in range(windows):
+            block = received_ref[owners_ref[window * tiles + t]].astype(F32)
+            term = weights_ref[window : window + 1, :] * block
+            total = term if total is None else total + term
+        video_ref[0, t * tile_pos : (t + 1) * tile_pos, :] = total.astype(BF16)
 
 
 def on_device(
@@ -215,17 +207,18 @@
     gathered = exchange(outgoing, FIRST)
 
     moved = (base_w, cond_w, gains, tconv, mlp_in, mlp_out)
-    projected, weights, zeros, spots, *params = pl.pallas_call(
+    projected, weights, zeros, spots, owners, *params = pl.pallas_call(
         functools.partial(side_kernel, tiles),
         out_shape=(
             VMEM((rows, channels), F32),
-            VMEM((count, tiles, channels), F32),
+            VMEM((windows, channels), F32),
             VMEM((count, tile_pos, channels), BF16),
             SMEM((2 * (window_len + 2),), jnp.int32),
+            SMEM((count,), jnp.int32),
             *(VMEM(array.shape, array.dtype) for array in moved),
         ),
         in_specs=[spec(SMEM)] * 3 + [spec(VMEM)] * 2 + [spec(pl.ANY)] * len(moved),
-        out_specs=(*(spec(VMEM),) * 3, spec(SMEM), *(spec(VMEM),) * len(moved)),
+        out_specs=(*(spec(VMEM),) * 3, *(spec(SMEM),) * 2, *(spec(VMEM),) * len(moved)),
         scratch_shapes=[
             SMEM((2 * count,), jnp.int32),
             pltpu.SemaphoreType.DMA((len(moved),)),
@@ -259,11 +252,11 @@
     return pl.pallas_call(
         blend_kernel,
         out_shape=jax.ShapeDtypeStruct((1, tiles * tile_pos, channels), BF16),
-        in_specs=[spec(VMEM)] * 2,
+        in_specs=[spec(SMEM)] + [spec(VMEM)] * 2,
         out_specs=spec(VMEM),
         compiler_params=pltpu.CompilerParams(vmem_limit_bytes=ROOM),
         name="blend",
-    )(*near(received, weights))
+    )(owners, *near(received, weights))
 
 
 def solution(mesh):

time: 25.6 us -> 25.5 us (level)
  no operation moved by 1% of the time
where the time goes in v8:
time: 25.5 us; the launch traced here: 25.1 us
  blocking collectives  10.2 us (40%)
  starting transfers between devices  7.79 us (31%)
  Pallas kernels  5.95 us (23%)
  waiting for transfers between devices  1.16 us (5%)
    all_to_all x1, blocking collectives, exchange(): lax.all_to_all(blocks, 'frame', split_axis=0, concat_axis=0, tiled=True,...  10.2 us
    all_to_all x1, starting transfers between devices, exchange(): lax.all_to_all(blocks, 'frame', split_axis=0, concat_axis=0, tiled=True,...  7.79 us
    pallas_call x1, Pallas kernels, on_device(): pl.pallas_call(functools.partial(side_kernel, tiles), out_shape=(VMEM((ro...  2.28 us
    pallas_call x1, Pallas kernels, on_device(): pl.pallas_call(refine_kernel, out_shape=VMEM((count, tile_pos, channels),...  1.58 us
    pallas_call x1, Pallas kernels, on_device(): pl.pallas_call(functools.partial(pick_kernel, tiles), out_shape=VMEM((cou...  1.4 us
    all_to_all x1, waiting for transfers between devices, exchange(): lax.all_to_all(blocks, 'frame', split_axis=0, concat_axis=0, tiled=True,...  1.16 us
    pallas_call x1, Pallas kernels, on_device(): pl.pallas_call(blend_kernel, out_shape=jax.ShapeDtypeStruct((1, tiles * t...  0.68 us
  transfers between devices with their start and end apart: 1, of which 1 were waited for; matrix products, arithmetic and copies ran while one was open for 0% of the time, Pallas kernels for 9%

profile of v8, /device:TPU:0, one launch (start us, length us, event | category | flops | bytes accessed | tf_op | source)
XLA Modules:
  0.0 25.1 jit_solution(17644012845058696168)
XLA Ops:
  0.0 1.4 %pick.1 = bf16[16,16,128]{2,1,0:T(8,128)(2,1)} custom-call(s32[16]{0:T(128)} %assign_ref.3, bf16[1,64,128]{2,1,0:T(8,128)(2,1)} %low_ref.1), custom_call_target="tpu_custom_call" | custom-call | tf_op jit(solution)/shard_map/pick/pallas_call | solution.py:199
  1.4 7.8 %all-to-all-start = ((bf16[16,16,128]{2,1,0:T(8,128)(2,1)}), bf16[16,16,128]{2,1,0:T(8,128)(2,1)S(1)}, u32[]{:S(2)}, u32[]{:S(2)}) async-start(bf16[16,16,128]{2,1,0:T(8,128)(2,1)} %pick.1), calls=%async_computation | async-start | bytes 131072 | tf_op jit(solution)/shard_map/all_to_all | solution.py:56
  9.2 2.3 %side.1 = (f32[512,128]{1,0:T(8,128)S(1)}, f32[4,128]{1,0:T(4,128)S(1)}, bf16[16,64,128]{2,1,0:T(8,128)(2,1)S(1)}, s32[20]{0:T(128)S(4)}, s32[16]{0:T(128)S(4)},...) custom-call(s32[16]{0:T(128)} %assign_ref.3, ...), custom_call_target="tpu_custom_call" | custom-call | flops 16777216 | bytes 262144 | tf_op jit(solution)/shard_map/side/pallas_call | solution.py:210
  11.5 1.2 %all-to-all-done.tile_ref = bf16[16,16,128]{2,1,0:T(8,128)(2,1)S(1)} async-done(((bf16[16,16,128]{2,1,0:T(8,128)(2,1)}), bf16[16,16,128]{2,1,0:T(8,128)(2,1)S(1)}, u32[]{:S(2)}, u32[]{:S(2)}) %all-to-all-start) | async-done | bytes 65568 | tf_op jit(solution)/shard_map/all_to_all | solution.py:56
  12.7 1.6 %refine.1 = bf16[16,64,128]{2,1,0:T(8,128)(2,1)S(1)} custom-call(s32[20]{0:T(128)S(4)} %get-tuple-element.17.spots_ref, bf16[16,16,128]{2,1,0:T(8,128)(2,1)S(1)} %all-to-all-done.tile_ref, f32[512,128]{1,0:T(8,128)S(1)} %get-tuple-element.18.projected_ref, bf16[3,128,128]{2,1,0:T(8,128)(2,1)S(1)} %get-tuple-element.19.base_w_ref, ...), custom_call_target="tpu_custom_call", output_to_operand_aliasing={{}: (9, {})} | custom-call | flops 402653184 | bytes 786432 | tf_op jit(solution)/shard_map/refine/pallas_call | solution.py:233
  14.2 10.2 %all_to_all.10.received_ref = bf16[16,64,128]{2,1,0:T(8,128)(2,1)S(1)} all-to-all(bf16[16,64,128]{2,1,0:T(8,128)(2,1)S(1)} %refine.1), channel_id=1, replica_groups={{11,10,4,8,13,6,15,0,7,1,5,12,9,3,2,14},{27,26,20,24,29,22,31,16,23,17,..., dimensions={0} | all-to-all | bytes 524288 | tf_op jit(solution)/shard_map/all_to_all | solution.py:56
  24.5 0.7 %blend.1 = bf16[1,256,128]{2,1,0:T(8,128)(2,1)} custom-call(s32[16]{0:T(128)S(4)} %get-tuple-element.16.owners_ref, bf16[16,64,128]{2,1,0:T(8,128)(2,1)S(1)} %all_to_all.10.received_ref, f32[4,128]{1,0:T(4,128)S(1)} %get-tuple-element.26.weights_ref), custom_call_target="tpu_custom_call" | custom-call | tf_op jit(solution)/shard_map/blend/pallas_call | solution.py:252
Async XLA Ops:
  1.4 11.2 %all-to-all-start = ((bf16[16,16,128]{2,1,0:T(8,128)(2,1)}), bf16[16,16,128]{2,1,0:T(8,128)(2,1)S(1)}, u32[]{:S(2)}, u32[]{:S(2)}) async-start(bf16[16,16,128]{2,1,0:T(8,128)(2,1)} %pick.1), calls=%async_computation | async-start | bytes 131072 | tf_op jit(solution)/shard_map/all_to_all | solution.py:56
